TPU v7x, 32 devices: a whole 2x2x4 slice. The times are simulated.
32 devices in a mesh: groups: 2 (over x), rows: 16 (over z, y, core).
Axes of the slice: x: 2, y: 2, z: 4, core: 2. Of those that a mesh axis runs over, the one named last changes fastest.
Arguments:
- coeffs: bfloat16 [1536, 8192], P(('groups', 'rows')), parts along dimension 0, may hold values from -0.0625 to 0.0625
- ham_blocks: bfloat16 [256, 16, 64, 64], P(('groups', 'rows')), parts along dimension 0, may hold values from -0.1875 to 0.1875
- metric_blocks: bfloat16 [256, 16, 64, 64], P(('groups', 'rows')), parts along dimension 0, may hold values from -0.0625 to 0.0625
- block_cols: int32 [256, 16], P(('groups', 'rows')), parts along dimension 0, may hold values from 0 to 127, as said below
- block_counts: int32 [256], P(('groups', 'rows')), parts along dimension 0, may hold values from 4 to 16, as said below
Outputs:
- gradient: bfloat16 [1536, 8192], P(('groups', 'rows')), parts along dimension 0
- band_hamiltonian: float32 [1536, 768], P('groups'), parts along dimension 0
- energy: float32 [2], P('groups'), parts along dimension 0
There are 2 independent parts, one for each index of `groups`. A program takes and returns all parts, laid end to end along the dimension named above; each array names one. Nothing has to cross between parts.
Inputs may be any that keep to these rules, and one draw needn't show every extreme that they name: `block_cols`: slot 0 of block row b holds b itself; every entry lies within 8 block rows of its own row. `block_counts`: slots of a row at or past its count are padding and their blocks are ignored; some row uses all 16 slots.
All inputs are finite; a program needn't handle non-finite values.
Results may differ from a plain program's by a relative error of at most 0.0078.
Values may be sent and summed in bfloat16 or wider, within the bound.
No kernel may reach another device: no remote copies, remote signals or barrier semaphores. Data moves between devices by JAX's collectives and lax.ppermute only.
A program may use at most 64 MiB of HBM per device.

v0:
```python
import math

import jax
import jax.numpy as jnp
from jax import lax
from jax.sharding import PartitionSpec as P


def with_halo(cells, sides, width):
    for axis, dim in sides:
        count = lax.axis_size(axis)
        ends = count - 1
        head = lax.slice_in_dim(cells, 0, width, axis=dim)
        tail = lax.slice_in_dim(cells, cells.shape[dim] - width, cells.shape[dim], axis=dim)
        cells = jnp.concatenate(
            [
                lax.ppermute(tail, axis, [(i, (i + 1) % count) for i in range(ends)]),
                cells,
                lax.ppermute(head, axis, [((i + 1) % count, i) for i in range(ends)]),
            ],
            axis=dim,
        )
    return cells


def local(coeffs, ham_blocks, metric_blocks, block_cols, block_counts):
    devices = lax.axis_size("rows")
    bands_dev, orbitals = coeffs.shape
    block_rows, slot_count, blocksz, _ = ham_blocks.shape
    row_span = block_rows * blocksz
    band_total = bands_dev * devices
    band_rows = coeffs.reshape(bands_dev, devices, row_span)
    own_cols = lax.all_to_all(band_rows, "rows", split_axis=1, concat_axis=0, tiled=True).reshape(
        band_total, row_span
    )
    wide_rows = with_halo(own_cols, (("rows", 1),), row_span)
    own_rows = wide_rows[:, row_span : 2 * row_span]
    offset_rows = lax.axis_index("rows") * block_rows - block_rows
    local_cols = block_cols - offset_rows
    stacked = wide_rows.reshape(band_total, 3 * block_rows, blocksz)
    row_mask = (jnp.arange(slot_count, dtype=jnp.int32)[None, :] < block_counts[:, None]).astype(
        jnp.bfloat16
    )[:, :, None, None]
    ham_masked = ham_blocks * row_mask
    metric_masked = metric_blocks * row_mask

    def apply_rows(step_index):
        offset = step_index * 2
        cols_part = lax.dynamic_slice_in_dim(local_cols, offset, 2, 0)
        ham_part = lax.dynamic_slice_in_dim(ham_masked, offset, 2, 0)
        metric_part = lax.dynamic_slice_in_dim(metric_masked, offset, 2, 0)
        picked = jnp.take(stacked, cols_part, axis=1)
        ham_out = jnp.einsum("jkrc,mjkc->mjr", ham_part, picked, preferred_element_type=jnp.float32)
        metric_out = jnp.einsum(
            "jkrc,mjkc->mjr", metric_part, picked, preferred_element_type=jnp.float32
        )
        return (ham_out, metric_out)

    ham_parts, metric_parts = lax.map(apply_rows, jnp.arange(block_rows // 2, dtype=jnp.int32))
    ham_prod = (
        jnp.transpose(ham_parts, (1, 0, 2, 3)).reshape(band_total, row_span).astype(jnp.bfloat16)
    )
    metric_full = jnp.transpose(metric_parts, (1, 0, 2, 3)).reshape(band_total, row_span)
    metric_prod = (own_rows.astype(jnp.float32) + metric_full).astype(jnp.bfloat16)

    def partial_gram(left_rows):
        return lax.dot_general(
            left_rows, own_rows, (((1,), (1,)), ((), ())), preferred_element_type=jnp.float32
        )

    ham_gram, metric_gram = lax.psum((partial_gram(ham_prod), partial_gram(metric_prod)), "rows")
    ham_band = ham_gram.astype(jnp.bfloat16)
    metric_band = metric_gram.astype(jnp.bfloat16)
    factor = math.sqrt(devices * row_span)
    ham_wide = ham_band.astype(jnp.float32)
    metric_wide = metric_band.astype(jnp.float32)
    band_hamiltonian = factor * ham_wide
    energy = factor * (2.0 * jnp.trace(ham_wide) - jnp.sum(metric_wide * ham_wide.T))
    grad_local = (
        4.0 * ham_prod.astype(jnp.float32)
        - 2.0 * jnp.dot(ham_band, metric_prod, preferred_element_type=jnp.float32)
        - 2.0 * jnp.dot(metric_band, ham_prod, preferred_element_type=jnp.float32)
    )
    grad_rows = (factor * grad_local).astype(jnp.bfloat16).reshape(devices, bands_dev, row_span)
    gradient = lax.all_to_all(grad_rows, "rows", split_axis=0, concat_axis=2, tiled=True).reshape(
        bands_dev, orbitals
    )
    return (gradient, band_hamiltonian, energy.reshape(1))


def solution(mesh):
    in_specs = (
        P(("groups", "rows"), None),
        P(("groups", "rows"), None, None, None),
        P(("groups", "rows"), None, None, None),
        P(("groups", "rows"), None),
        P(("groups", "rows")),
    )
    out_specs = (P(("groups", "rows"), None), P("groups", None), P("groups"))
    return jax.shard_map(local, mesh=mesh, in_specs=in_specs, out_specs=out_specs, check_vma=False)
```

profile of v0, /device:TPU:9, one launch (start us, length us, event | category | flops | bytes accessed | tf_op | source)
XLA Modules:
  0.0 248.2 jit_solution(327089912878135035)
XLA Ops:
  0.6 0.0 copy-start.5
  0.6 0.0 copy-start.6
  0.7 0.0 copy-start.2
  0.7 2.2 copy.50
  2.9 6.6 %all-to-all-start = ((bf16[48,16,512]{2,0,1:T(8,128)(2,1)}), bf16[48,16,512]{2,0,1:T(8,128)(2,1)S(1)}, u32[]{:S(2)}, u32[]{:S(2)}) async-start(bf16[48,16,512]{2,0,1:T(8,128)(2,1)} %bitcast.85), calls=%async_computation | async-start | bytes 1572864 | tf_op jit(solution)/shard_map/all_to_all | solution.py:33
  9.5 0.0 copy-done.5
  9.5 19.5 %all-to-all-done = bf16[48,16,512]{2,0,1:T(8,128)(2,1)S(1)} async-done(((bf16[48,16,512]{2,0,1:T(8,128)(2,1)}), bf16[48,16,512]{2,0,1:T(8,128)(2,1)S(1)}, u32[]{:S(2)}, u32[]{:S(2)}) %all-to-all-start) | async-done | bytes 786464 | tf_op jit(solution)/shard_map/all_to_all | solution.py:33
  29.1 2.9 %collective-permute-start = (bf16[768,512]{1,0:T(8,128)(2,1)S(1)}, bf16[768,512]{1,0:T(8,128)(2,1)}, u32[]{:S(2)}, u32[]{:S(2)}) collective-permute-start(bf16[768,512]{1,0:T(8,128)(2,1)S(1)} %bitcast.100), channel_id=1, source_target_pairs={{0,1},{1,2},{2,3},{3,4},{4,5},{5,6},{6,7},{7,8},{8,9},{9,10},{10,1... | collective-permute-start | bytes 2359304 | tf_op jit(solution)/shard_map/ppermute | solution.py:17
  31.9 1.9 collective-permute-start.1
  33.9 0.0 copy-done.6
  33.9 0.1 fusion.30
  34.0 0.0 copy-done.2
  34.0 4.0 %broadcast_multiply_fusion = (bf16[8,16,64,64]{3,2,1,0:T(8,128)(2,1)}, bf16[8,16,64,64]{3,2,1,0:T(8,128)(2,1)}) fusion(bf16[8,16,64,64]{3,2,1,0:T(8,128)(2,1)S(1)} %copy-done.2, bf16[8,16]{1,0:T(8,128)(2,1)S(1)} %fusion.30, bf16[8,16,64,64]{3,2,1,0:T(8,128)(2,1)} %param.8), kind=kLoop, calls=%fused_computation.34 | loop fusion | flops 1048576 | bytes 4194560 | tf_op jit(solution)/shard_map/mul | solution.py:45
  37.9 0.8 concatenate.11
  38.7 1.7 copy.37
  40.5 0.2 bitcast_convert_fusion
  40.7 3.4 %reshape.73 = f32[768,4,2,64]{3,2,1,0:T(2,128)} reshape(f32[16,48,1,512]{3,1,0,2:T(8,128)S(1)} %bitcast_convert_fusion) | data formatting | bytes 3145728 | tf_op jit(solution)/shard_map/convert_element_type | solution.py:64
  44.1 5.4 %copy.40 = f32[768,4,2,64]{0,3,2,1:T(8,128)} copy(f32[768,4,2,64]{3,2,1,0:T(2,128)} %reshape.73) | data formatting | bytes 3145728 | tf_op jit(solution)/shard_map/convert_element_type | solution.py:64
  49.5 0.0 collective-permute-done
  49.5 2.3 copy.35
  51.8 0.0 collective-permute-done.1
  51.8 2.3 copy.36
  54.1 1.9 pad_maximum_fusion
  55.9 40.9 %while.12 = (s32[]{:T(128)}, bf16[4,768,2,64]{1,3,2,0:T(8,128)(2,1)}, f32[4,768,2,64]{1,3,2,0:T(8,128)}, s32[4]{0:T(128)S(1)}, s32[8,16]{1,0:T(8,128)S(1)}, /*in...) while((s32[]{:T(128)}, ...), condition=%wide.region_1.2_spmd, body=%wide.region_0.1_spmd.sunk | while | flops 405800128 | bytes 27007032 | solution.py:59
  56.0 0.6 dynamic_slice.26
  57.2 0.1 reshape.91
  57.3 2.4 gather_fusion
  59.7 3.8 %fusion.51 = f32[4,768,2,64]{1,3,2,0:T(8,128)} fusion(f32[4,768,2,64]{1,3,2,0:T(8,128)} %get-tuple-element.139, s32[]{:T(128)} %get-tuple-element.137, bf16[2,16,768,64]{2,3,1,0:T(8,128)(2,1)} %bitcast.98, pred[2,16]{1,0:T(4,128)(4,1)S(1)} %get-tuple-element.124, bf16[8,16,64,64]{3,2,1,0:T(8,128)(2,1)} %get-tuple-element.156, s32[]{:T(128)S(6)} %select_n.46), kind=kOutput, calls=%fused_computation.9.clone.1 | convolution fusion | flops 202899456 | bytes 4063780 | tf_op jit(solution)/shard_map/while/body/eval_jaxpr/jkrc,mjkc->mjr/dot_general | solution.py:54
  63.6 0.0 copy-done
  63.6 2.6 %fusion.50 = bf16[4,768,2,64]{1,3,2,0:T(8,128)(2,1)} fusion(bf16[4,768,2,64]{1,3,2,0:T(8,128)(2,1)} %get-tuple-element.138, s32[]{:T(128)} %get-tuple-element.137, bf16[2,16,768,64]{2,3,1,0:T(8,128)(2,1)S(1)} %bitcast.99, pred[2,16]{1,0:T(4,128)(4,1)S(1)} %get-tuple-element.124, bf16[8,16,64,64]{3,2,1,0:T(8,128)(2,1)} %get-tuple-element.155, ...), kind=kOutput, calls=%fused_computation.11.clone.1 | convolution fusion | flops 202899456 | bytes 4063780 | tf_op jit(solution)/shard_map/while/body/eval_jaxpr/jkrc,mjkc->mjr/dot_general | solution.py:53
  66.2 0.6 dynamic_slice.26
  67.5 0.1 reshape.91
  67.6 2.4 gather_fusion
  70.0 3.8 %fusion.51 = f32[4,768,2,64]{1,3,2,0:T(8,128)} fusion(f32[4,768,2,64]{1,3,2,0:T(8,128)} %get-tuple-element.139, s32[]{:T(128)} %get-tuple-element.137, bf16[2,16,768,64]{2,3,1,0:T(8,128)(2,1)} %bitcast.98, pred[2,16]{1,0:T(4,128)(4,1)S(1)} %get-tuple-element.124, bf16[8,16,64,64]{3,2,1,0:T(8,128)(2,1)} %get-tuple-element.156, s32[]{:T(128)S(6)} %select_n.46), kind=kOutput, calls=%fused_computation.9.clone.1 | convolution fusion | flops 202899456 | bytes 4063780 | tf_op jit(solution)/shard_map/while/body/eval_jaxpr/jkrc,mjkc->mjr/dot_general | solution.py:54
  73.8 0.0 copy-done
  73.8 2.6 %fusion.50 = bf16[4,768,2,64]{1,3,2,0:T(8,128)(2,1)} fusion(bf16[4,768,2,64]{1,3,2,0:T(8,128)(2,1)} %get-tuple-element.138, s32[]{:T(128)} %get-tuple-element.137, bf16[2,16,768,64]{2,3,1,0:T(8,128)(2,1)S(1)} %bitcast.99, pred[2,16]{1,0:T(4,128)(4,1)S(1)} %get-tuple-element.124, bf16[8,16,64,64]{3,2,1,0:T(8,128)(2,1)} %get-tuple-element.155, ...), kind=kOutput, calls=%fused_computation.11.clone.1 | convolution fusion | flops 202899456 | bytes 4063780 | tf_op jit(solution)/shard_map/while/body/eval_jaxpr/jkrc,mjkc->mjr/dot_general | solution.py:53
  76.4 0.6 dynamic_slice.26
  77.7 0.1 reshape.91
  77.8 2.4 gather_fusion
  80.2 3.8 %fusion.51 = f32[4,768,2,64]{1,3,2,0:T(8,128)} fusion(f32[4,768,2,64]{1,3,2,0:T(8,128)} %get-tuple-element.139, s32[]{:T(128)} %get-tuple-element.137, bf16[2,16,768,64]{2,3,1,0:T(8,128)(2,1)} %bitcast.98, pred[2,16]{1,0:T(4,128)(4,1)S(1)} %get-tuple-element.124, bf16[8,16,64,64]{3,2,1,0:T(8,128)(2,1)} %get-tuple-element.156, s32[]{:T(128)S(6)} %select_n.46), kind=kOutput, calls=%fused_computation.9.clone.1 | convolution fusion | flops 202899456 | bytes 4063780 | tf_op jit(solution)/shard_map/while/body/eval_jaxpr/jkrc,mjkc->mjr/dot_general | solution.py:54
  84.0 0.0 copy-done
  84.0 2.6 %fusion.50 = bf16[4,768,2,64]{1,3,2,0:T(8,128)(2,1)} fusion(bf16[4,768,2,64]{1,3,2,0:T(8,128)(2,1)} %get-tuple-element.138, s32[]{:T(128)} %get-tuple-element.137, bf16[2,16,768,64]{2,3,1,0:T(8,128)(2,1)S(1)} %bitcast.99, pred[2,16]{1,0:T(4,128)(4,1)S(1)} %get-tuple-element.124, bf16[8,16,64,64]{3,2,1,0:T(8,128)(2,1)} %get-tuple-element.155, ...), kind=kOutput, calls=%fused_computation.11.clone.1 | convolution fusion | flops 202899456 | bytes 4063780 | tf_op jit(solution)/shard_map/while/body/eval_jaxpr/jkrc,mjkc->mjr/dot_general | solution.py:53
  86.6 0.6 dynamic_slice.26
  87.9 0.1 reshape.91
  88.0 2.4 gather_fusion
  90.4 3.9 %fusion.51 = f32[4,768,2,64]{1,3,2,0:T(8,128)} fusion(f32[4,768,2,64]{1,3,2,0:T(8,128)} %get-tuple-element.139, s32[]{:T(128)} %get-tuple-element.137, bf16[2,16,768,64]{2,3,1,0:T(8,128)(2,1)} %bitcast.98, pred[2,16]{1,0:T(4,128)(4,1)S(1)} %get-tuple-element.124, bf16[8,16,64,64]{3,2,1,0:T(8,128)(2,1)} %get-tuple-element.156, s32[]{:T(128)S(6)} %select_n.46), kind=kOutput, calls=%fused_computation.9.clone.1 | convolution fusion | flops 202899456 | bytes 4063780 | tf_op jit(solution)/shard_map/while/body/eval_jaxpr/jkrc,mjkc->mjr/dot_general | solution.py:54
  94.2 0.0 copy-done
  94.2 2.6 %fusion.50 = bf16[4,768,2,64]{1,3,2,0:T(8,128)(2,1)} fusion(bf16[4,768,2,64]{1,3,2,0:T(8,128)(2,1)} %get-tuple-element.138, s32[]{:T(128)} %get-tuple-element.137, bf16[2,16,768,64]{2,3,1,0:T(8,128)(2,1)S(1)} %bitcast.99, pred[2,16]{1,0:T(4,128)(4,1)S(1)} %get-tuple-element.124, bf16[8,16,64,64]{3,2,1,0:T(8,128)(2,1)} %get-tuple-element.155, ...), kind=kOutput, calls=%fused_computation.11.clone.1 | convolution fusion | flops 202899456 | bytes 4063780 | tf_op jit(solution)/shard_map/while/body/eval_jaxpr/jkrc,mjkc->mjr/dot_general | solution.py:53
  96.9 2.0 fusion.31
  98.8 2.3 copy.38
  101.1 2.0 fusion.27
  103.2 2.2 fusion.32
  105.3 3.0 %copy.39 = f32[768,512]{1,0:T(8,128)} copy(f32[768,512]{0,1:T(8,128)} %bitcast.106) | data formatting | bytes 3145728 | tf_op jit(solution)/shard_map/reshape | solution.py:63
  108.4 108.0 %all-reduce.2 = (bf16[768,768]{1,0:T(8,128)(2,1)}, bf16[768,768]{0,1:T(8,128)(2,1)}) all-reduce(f32[768,768]{1,0:T(8,128)S(1)} %fusion.31, f32[768,768]{0,1:T(8,128)} %fusion.32), channel_id=1, replica_groups=mesh['groups'=2,'rows'=16] {'rows'}, use_global_device_ids=true, to_apply=%region_2.3 | all-reduce | flops 1179648 | bytes 7077888 | tf_op jit(solution)/shard_map/psum | solution.py:71
  216.4 2.7 %fusion.28 = f32[768,512]{1,0:T(8,128)S(1)} fusion(bf16[768,768]{1,0:T(8,128)(2,1)} %get-tuple-element.64, f32[768,512]{1,0:T(8,128)} %copy.39, bf16[768,512]{1,0:T(8,128)(2,1)S(1)} %bitcast.105), kind=kOutput, calls=%fused_computation.36 | convolution fusion | flops 605159424 | bytes 5111808 | tf_op jit(solution)/shard_map/dot_general | solution.py:81
  219.1 0.0 copy-done.3
  219.1 0.0 copy-done.4
  219.1 3.0 %multiply_convert_fusion = bf16[768,512]{1,0:T(8,128)(2,1)} fusion(f32[768,512]{1,0:T(8,128)S(1)} %fusion.28, bf16[768,512]{1,0:T(8,128)(2,1)S(1)} %copy-done.4, bf16[768,512]{0,1:T(8,128)(2,1)} %bitcast.19, bf16[768,768]{0,1:T(8,128)(2,1)S(1)} %copy-done.3), kind=kOutput, calls=%fused_computation.32 | convolution fusion | flops 607125504 | bytes 5111808 | tf_op jit(solution)/shard_map/dot_general | solution.py:82
  222.1 4.4 %all-to-all-start.1 = ((bf16[16,48,512]{2,1,0:T(8,128)(2,1)}), bf16[16,48,512]{2,1,0:T(8,128)(2,1)S(1)}, u32[]{:S(2)}, u32[]{:S(2)}) async-start(bf16[16,48,512]{2,1,0:T(8,128)(2,1)} %bitcast.112), calls=%async_computation.1 | async-start | bytes 1572864 | tf_op jit(solution)/shard_map/all_to_all | solution.py:85
  226.5 0.0 copy-done.1
  226.5 2.2 fusion.24
  229.4 1.2 fusion.26
  231.3 14.8 %all-to-all-done.1 = bf16[16,48,512]{2,1,0:T(8,128)(2,1)S(1)} async-done(((bf16[16,48,512]{2,1,0:T(8,128)(2,1)}), bf16[16,48,512]{2,1,0:T(8,128)(2,1)S(1)}, u32[]{:S(2)}, u32[]{:S(2)}) %all-to-all-start.1) | async-done | bytes 786464 | tf_op jit(solution)/shard_map/all_to_all | solution.py:85
  246.1 1.0 copy.47
  (19 shorter events, 0.1 us)
Async XLA Ops:
  0.6 8.9 %copy-start.5 = (s32[8,16]{1,0:T(8,128)S(1)}, s32[8,16]{1,0:T(8,128)}, u32[]{:S(2)}) copy-start(s32[8,16]{1,0:T(8,128)} %param.10) | copy-start | bytes 1540
  0.6 33.2 %copy-start.6 = (s32[8]{0:T(128)S(1)}, s32[8]{0:T(128)}, u32[]{:S(2)}) copy-start(s32[8]{0:T(128)} %param.11) | copy-start | bytes 100
  0.7 33.3 %copy-start.2 = (bf16[8,16,64,64]{3,2,1,0:T(8,128)(2,1)S(1)}, bf16[8,16,64,64]{3,2,1,0:T(8,128)(2,1)}, u32[]{:S(2)}) copy-start(bf16[8,16,64,64]{3,2,1,0:T(8,128)(2,1)} %param.9) | copy-start | bytes 3145732
  2.9 26.2 %all-to-all-start = ((bf16[48,16,512]{2,0,1:T(8,128)(2,1)}), bf16[48,16,512]{2,0,1:T(8,128)(2,1)S(1)}, u32[]{:S(2)}, u32[]{:S(2)}) async-start(bf16[48,16,512]{2,0,1:T(8,128)(2,1)} %bitcast.85), calls=%async_computation | async-start | bytes 1572864 | tf_op jit(solution)/shard_map/all_to_all | solution.py:33
  29.1 20.4 %collective-permute-start = (bf16[768,512]{1,0:T(8,128)(2,1)S(1)}, bf16[768,512]{1,0:T(8,128)(2,1)}, u32[]{:S(2)}, u32[]{:S(2)}) collective-permute-start(bf16[768,512]{1,0:T(8,128)(2,1)S(1)} %bitcast.100), channel_id=1, source_target_pairs={{0,1},{1,2},{2,3},{3,4},{4,5},{5,6},{6,7},{7,8},{8,9},{9,10},{10,1... | collective-permute-start | bytes 2359304 | tf_op jit(solution)/shard_map/ppermute | solution.py:17
  31.9 19.8 %collective-permute-start.1 = (bf16[768,512]{1,0:T(8,128)(2,1)S(1)}, bf16[768,512]{1,0:T(8,128)(2,1)}, u32[]{:S(2)}, u32[]{:S(2)}) collective-permute-start(bf16[768,512]{1,0:T(8,128)(2,1)S(1)} %bitcast.101), channel_id=1, source_target_pairs={{1,0},{2,1},{3,2},{4,3},{5,4},{6,5},{7,6},{8,7},{9,8},{10,9},{11,1... | collective-permute-start | bytes 2359304 | tf_op jit(solution)/shard_map/ppermute | solution.py:19
  59.7 3.9 %copy-start = (bf16[32,768,64]{1,2,0:T(8,128)(2,1)S(1)}, bf16[32,768,64]{1,2,0:T(8,128)(2,1)}, u32[]{:S(2)}) copy-start(bf16[32,768,64]{1,2,0:T(8,128)(2,1)} %gather_fusion) | copy-start | bytes 9437188 | tf_op jit(solution)/shard_map/while
  70.0 3.8 %copy-start = (bf16[32,768,64]{1,2,0:T(8,128)(2,1)S(1)}, bf16[32,768,64]{1,2,0:T(8,128)(2,1)}, u32[]{:S(2)}) copy-start(bf16[32,768,64]{1,2,0:T(8,128)(2,1)} %gather_fusion) | copy-start | bytes 9437188 | tf_op jit(solution)/shard_map/while
  80.2 3.8 %copy-start = (bf16[32,768,64]{1,2,0:T(8,128)(2,1)S(1)}, bf16[32,768,64]{1,2,0:T(8,128)(2,1)}, u32[]{:S(2)}) copy-start(bf16[32,768,64]{1,2,0:T(8,128)(2,1)} %gather_fusion) | copy-start | bytes 9437188 | tf_op jit(solution)/shard_map/while
  90.4 3.9 %copy-start = (bf16[32,768,64]{1,2,0:T(8,128)(2,1)S(1)}, bf16[32,768,64]{1,2,0:T(8,128)(2,1)}, u32[]{:S(2)}) copy-start(bf16[32,768,64]{1,2,0:T(8,128)(2,1)} %gather_fusion) | copy-start | bytes 9437188 | tf_op jit(solution)/shard_map/while
  216.4 2.7 %copy-start.3 = (bf16[768,768]{0,1:T(8,128)(2,1)S(1)}, bf16[768,768]{0,1:T(8,128)(2,1)}, u32[]{:S(2)}) copy-start(bf16[768,768]{0,1:T(8,128)(2,1)} %get-tuple-element.65) | copy-start | bytes 3538948
  216.4 2.7 %copy-start.4 = (bf16[768,512]{1,0:T(8,128)(2,1)S(1)}, bf16[768,512]{1,0:T(8,128)(2,1)}, u32[]{:S(2)}) copy-start(bf16[768,512]{1,0:T(8,128)(2,1)} %copy.38) | copy-start | bytes 2359300
  222.1 4.4 %copy-start.1 = (bf16[768,768]{1,0:T(8,128)(2,1)S(1)}, bf16[768,768]{1,0:T(8,128)(2,1)}, u32[]{:S(2)}) copy-start(bf16[768,768]{1,0:T(8,128)(2,1)} %get-tuple-element.64) | copy-start | bytes 3538948
  222.1 24.0 %all-to-all-start.1 = ((bf16[16,48,512]{2,1,0:T(8,128)(2,1)}), bf16[16,48,512]{2,1,0:T(8,128)(2,1)S(1)}, u32[]{:S(2)}, u32[]{:S(2)}) async-start(bf16[16,48,512]{2,1,0:T(8,128)(2,1)} %bitcast.112), calls=%async_computation.1 | async-start | bytes 1572864 | tf_op jit(solution)/shard_map/all_to_all | solution.py:85
where the time goes:
time: 249 us; the launch traced here: 248 us
  blocking collectives  108 us (43%)
  local copies, waits for them, and re-layouts  36.9 us (15%)
  matrix products  35.6 us (14%)
  waiting for transfers between devices  34.3 us (14%)
  starting transfers between devices  15.8 us (6%)
  other arithmetic  11.7 us (5%)
  between operations  3.2 us (1%)
  loops' own time  2.6 us (1%)
    psum x1, blocking collectives, local(): lax.psum((partial_gram(ham_prod), partial_gram(metric_prod)), 'rows')  108 us
    all_to_all x1, waiting for transfers between devices, local(): lax.all_to_all(band_rows, 'rows', split_axis=1, concat_axis=0, tiled=True)  19.5 us
    dot_general x4, matrix products, apply_rows(): jnp.einsum('jkrc,mjkc->mjr', metric_part, picked, preferred_element_type=...  15.4 us
    all_to_all x1, waiting for transfers between devices, local(): lax.all_to_all(grad_rows, 'rows', split_axis=0, concat_axis=2, tiled=True)  14.8 us
    dot_general x4, matrix products, apply_rows(): jnp.einsum('jkrc,mjkc->mjr', ham_part, picked, preferred_element_type=jnp...  10.5 us
    gather x4, local copies, waits for them, and re-layouts, apply_rows(): picked = jnp.take(stacked, cols_part, axis=1)  9.53 us
    convert_element_type x2, local copies, waits for them, and re-layouts, local(): own_rows.astype(jnp.float32) + metric_full  8.82 us
    all_to_all x1, starting transfers between devices, local(): lax.all_to_all(band_rows, 'rows', split_axis=1, concat_axis=0, tiled=True)  6.61 us
  transfers between devices with their start and end apart: 4, of which 2 were waited for; matrix products, arithmetic and copies ran while one was open for 9% of the time, Pallas kernels for 0%

commit v1 on v0

v1 whole, which is shorter than its diff:
```python
import functools
import math

import jax
import jax.numpy as jnp
from jax import lax
from jax.experimental import pallas as pl
from jax.experimental.pallas import tpu as pltpu
from jax.sharding import PartitionSpec as P

NT = (((1,), (1,)), ((), ()))


def nt_dot(left, right):
    return lax.dot_general(left, right, NT, preferred_element_type=jnp.float32)


def expand_kernel(cols_ref, counts_ref, ham_ref, metric_ref, wide_ref, acc_ref):
    row = pl.program_id(0)
    slots, size = ham_ref.shape[1], ham_ref.shape[2]
    acc_ref[...] = jnp.zeros_like(acc_ref)
    half = lax.broadcasted_iota(jnp.int32, (size, 2 * size), 1) // size
    for slot in range(slots):
        col = cols_ref[row, slot]
        want = jnp.where(slot < counts_ref[row], col % 2, 2)
        keep = half == want
        lanes = pl.ds(pl.multiple_of((col // 2) * 2 * size, 2 * size), 2 * size)
        for which, blocks in enumerate((ham_ref, metric_ref)):
            block = blocks[0, slot].astype(jnp.float32)
            twice = jnp.concatenate([block, block], axis=1)
            acc_ref[which, :, lanes] += jnp.where(keep, twice, 0.0)
    wide_ref[...] = acc_ref[...].astype(wide_ref.dtype)


def expand(cols, counts, ham_blocks, metric_blocks):
    rows, slots, size, _ = ham_blocks.shape
    width = 3 * rows * size
    blocks_spec = pl.BlockSpec((1, slots, size, size), lambda b, *_: (b, 0, 0, 0))
    return pl.pallas_call(
        expand_kernel,
        out_shape=jax.ShapeDtypeStruct((2, rows * size, width), jnp.bfloat16),
        grid_spec=pltpu.PrefetchScalarGridSpec(
            num_scalar_prefetch=2,
            grid=(rows,),
            in_specs=[blocks_spec, blocks_spec],
            out_specs=pl.BlockSpec((2, size, width), lambda b, *_: (0, b, 0)),
            scratch_shapes=[pltpu.VMEM((2, size, width), jnp.float32)],
        ),
        compiler_params=pltpu.CompilerParams(vmem_limit_bytes=16 * 2**20),
        cost_estimate=pl.CostEstimate(
            flops=2 * ham_blocks.size, bytes_accessed=16 * 2**20, transcendentals=0
        ),
        name="expand",
    )(cols, counts, ham_blocks, metric_blocks)


def product_kernel(left_ref, own_ref, right_ref, all_ref, wide_ref, ham_ref, metric_ref, ham_gram_ref, metric_gram_ref):
    span = own_ref.shape[1]
    own = own_ref[...]

    def apply(which):
        total = nt_dot(own, wide_ref[which, :, span : 2 * span])
        total += nt_dot(left_ref[...], wide_ref[which, :, :span])
        return total + nt_dot(right_ref[...], wide_ref[which, :, 2 * span :])

    ham = apply(0).astype(jnp.bfloat16)
    metric = (own.astype(jnp.float32) + apply(1)).astype(jnp.bfloat16)
    ham_ref[...] = ham
    metric_ref[...] = metric
    ham_gram_ref[...] = nt_dot(ham, all_ref[...])
    metric_gram_ref[...] = nt_dot(metric, all_ref[...])


def product(left, own, right, wide, steps=2):
    bands, span = own.shape
    rows = bands // steps
    part = pl.BlockSpec((rows, span), lambda i, *_: (i, 0))
    square = pl.BlockSpec((rows, bands), lambda i, *_: (i, 0))
    return pl.pallas_call(
        product_kernel,
        out_shape=(
            jax.ShapeDtypeStruct((bands, span), jnp.bfloat16),
            jax.ShapeDtypeStruct((bands, span), jnp.bfloat16),
            jax.ShapeDtypeStruct((bands, bands), jnp.float32),
            jax.ShapeDtypeStruct((bands, bands), jnp.float32),
        ),
        grid_spec=pl.GridSpec(
            grid=(steps,),
            in_specs=[
                part,
                part,
                part,
                pl.BlockSpec((bands, span), lambda i, *_: (0, 0)),
                pl.BlockSpec(wide.shape, lambda i, *_: (0, 0, 0)),
            ],
            out_specs=[part, part, square, square],
        ),
        compiler_params=pltpu.CompilerParams(vmem_limit_bytes=32 * 2**20),
        cost_estimate=pl.CostEstimate(
            flops=2 * bands * span * (6 * span + 2 * bands), bytes_accessed=13 * 2**20, transcendentals=0
        ),
        name="product",
    )(left, own, right, own, wide)


def gradient_kernel(factor, ham_band_ref, metric_band_ref, part_ref, ham_ref, metric_ref, out_ref):
    total = jnp.dot(ham_band_ref[...], metric_ref[...], preferred_element_type=jnp.float32)
    total += jnp.dot(metric_band_ref[...], ham_ref[...], preferred_element_type=jnp.float32)
    out_ref[...] = (factor * (4.0 * part_ref[...].astype(jnp.float32) - 2.0 * total)).astype(jnp.bfloat16)


def gradient_of(factor, ham_band, metric_band, ham_prod, metric_prod, steps=2):
    bands, span = ham_prod.shape
    rows = bands // steps
    square = pl.BlockSpec((rows, bands), lambda i, *_: (i, 0))
    part = pl.BlockSpec((rows, span), lambda i, *_: (i, 0))
    whole = pl.BlockSpec((bands, span), lambda i, *_: (0, 0))
    return pl.pallas_call(
        functools.partial(gradient_kernel, factor),
        out_shape=jax.ShapeDtypeStruct((bands, span), jnp.bfloat16),
        grid_spec=pl.GridSpec(
            grid=(steps,),
            in_specs=[square, square, part, whole, whole],
            out_specs=part,
        ),
        compiler_params=pltpu.CompilerParams(vmem_limit_bytes=24 * 2**20),
        cost_estimate=pl.CostEstimate(
            flops=4 * bands * bands * span, bytes_accessed=6 * 2**20, transcendentals=0
        ),
        name="gradient",
    )(ham_band, metric_band, ham_prod, ham_prod, metric_prod)


def swap(value, bit):
    count = lax.axis_size("rows")
    return lax.ppermute(value, "rows", [(i, i ^ bit) for i in range(count)])


def fill_row(cols, blocks_of, acc_ref, size):
    half = lax.broadcasted_iota(jnp.int32, (size, 2 * size), 1) // size
    for slot, col in enumerate(cols):
        want = jnp.where(col < 0, 2, col % 2)
        lanes = at_block(jnp.maximum(col, 0) // 2, 2 * size)
        for which, block in enumerate(blocks_of(slot)):
            block = block.astype(jnp.float32)
            twice = jnp.concatenate([block, block], axis=1)
            acc_ref[which, :, lanes] += jnp.where(half == want, twice, 0.0)


def write_levels(acc_ref, inner_ref, outer_ref):
    total = acc_ref[...]
    high = total.astype(jnp.bfloat16)
    low = (total - high.astype(jnp.float32)).astype(jnp.bfloat16)
    width = inner_ref.shape[-1]
    for level, value in enumerate((high, low)):
        inner_ref[level] = value[:, :, :width]
        outer_ref[level] = value[:, :, width:]


def expand_own_kernel(cols_ref, ham_ref, metric_ref, inner_ref, outer_ref, packed_ref, acc_ref):
    row = pl.program_id(0)
    slots, size = ham_ref.shape[1], ham_ref.shape[2]
    acc_ref[...] = jnp.zeros_like(acc_ref)
    cols = [cols_ref[row, slot] for slot in range(slots)]
    fill_row(cols, lambda slot: (ham_ref[0, slot], metric_ref[0, slot]), acc_ref, size)
    write_levels(acc_ref, inner_ref, outer_ref)
    for which, blocks_ref in enumerate((ham_ref, metric_ref)):
        for slot in range(slots // 2):
            both = jnp.concatenate([blocks_ref[0, slot], blocks_ref[0, slot + slots // 2]], axis=1)
            packed_ref[which, 0, slot] = both


def expand_packed_kernel(cols_ref, packed_ref, inner_ref, outer_ref, acc_ref):
    row = pl.program_id(0)
    pairs, size = packed_ref.shape[2], packed_ref.shape[3]
    acc_ref[...] = jnp.zeros_like(acc_ref)

    def blocks_of(slot):
        lanes = slice(0, size) if slot < pairs else slice(size, 2 * size)
        return [packed_ref[which, 0, slot % pairs][:, lanes] for which in range(2)]

    fill_row([cols_ref[row, slot] for slot in range(2 * pairs)], blocks_of, acc_ref, size)
    write_levels(acc_ref, inner_ref, outer_ref)


def expand_call(cols, *blocks):
    rows, slots = cols.shape
    size = blocks[0].shape[3]
    span = rows * size
    packed = jax.ShapeDtypeStruct((2, rows, slots // 2, size, 2 * size), jnp.bfloat16)
    packed_spec = pl.BlockSpec((2, 1, slots // 2, size, 2 * size), lambda b, *_: (0, b, 0, 0, 0))
    blocks_spec = pl.BlockSpec((1, slots, size, size), lambda b, *_: (b, 0, 0, 0))
    own = len(blocks) == 2
    return pl.pallas_call(
        expand_own_kernel if own else expand_packed_kernel,
        out_shape=[
            jax.ShapeDtypeStruct((2, 2, span, 2 * span), jnp.bfloat16),
            jax.ShapeDtypeStruct((2, 2, span, span), jnp.bfloat16),
        ]
        + [packed] * own,
        grid_spec=pltpu.PrefetchScalarGridSpec(
            num_scalar_prefetch=1,
            grid=(rows,),
            in_specs=[blocks_spec, blocks_spec] if own else [packed_spec],
            out_specs=[
                pl.BlockSpec((2, 2, size, 2 * span), lambda b, *_: (0, 0, b, 0)),
                pl.BlockSpec((2, 2, size, span), lambda b, *_: (0, 0, b, 0)),
            ]
            + [packed_spec] * own,
            scratch_shapes=[pltpu.VMEM((2, size, 3 * span), jnp.float32)],
        ),
        compiler_params=pltpu.CompilerParams(vmem_limit_bytes=16 * 2**20),
        cost_estimate=pl.CostEstimate(flops=0, bytes_accessed=1024, transcendentals=0),
        name="expand_own" if own else "expand_packed",
    )(cols, *blocks)


def tie(value, *before):
    return lax.optimization_barrier((value, *before))[0]


def at_block(block, piece):
    return pl.ds(pl.multiple_of(block * piece, piece), piece)


def whole_call(kernel, name, outs, scratch=(), limit=8):
    vmem, smem = pl.BlockSpec(memory_space=pltpu.VMEM), pl.BlockSpec(memory_space=pltpu.SMEM)

    def call(scalars, *args):
        return pl.pallas_call(
            kernel,
            out_shape=tuple(jax.ShapeDtypeStruct(shape, dtype) for shape, dtype in outs),
            in_specs=[smem] + [vmem] * len(args),
            out_specs=tuple(smem if shape == (1, 1) else vmem for shape, _ in outs),
            scratch_shapes=scratch,
            compiler_params=pltpu.CompilerParams(vmem_limit_bytes=limit * 2**20),
            cost_estimate=pl.CostEstimate(flops=0, bytes_accessed=1024, transcendentals=0),
            name=name,
        )(scalars, *args)

    return call


def split_kernel(place_ref, coeffs_ref, *out_refs):
    width = out_refs[0].shape[1]
    for step, out_ref in enumerate(out_refs):
        out_ref[...] = coeffs_ref[:, at_block(place_ref[0] ^ step, width)]


def join_kernel(place_ref, *refs):
    *part_refs, out_ref = refs
    width = part_refs[0].shape[1]
    for step, part_ref in enumerate(part_refs):
        out_ref[:, at_block(place_ref[0] ^ step, width)] = part_ref[...]


def stack_kernel(place_ref, *refs):
    *part_refs, out_ref, low_ref, high_ref = refs
    piece, width = part_refs[0].shape
    for step, part_ref in enumerate(part_refs):
        rows = at_block(place_ref[0] ^ step, piece)
        part = part_ref[...]
        out_ref[rows, :] = part
        low_ref[rows, :] = part[:, : width // 2]
        high_ref[rows, :] = part[:, width // 2 :]


def inner_kernel(piece, place_ref, own_ref, cross_ref, mine_ref, other_ref, all_ref, sums_ref):
    core = place_ref[1]
    rows, width = own_ref.shape
    span = width // 2
    for chip in range(rows // piece):
        source = pl.ds(chip * piece, piece)
        all_ref[at_block(2 * chip + core, piece), :] = own_ref[source, :]
        all_ref[at_block(2 * chip + 1 - core, piece), :] = cross_ref[source, :]
    own = own_ref[...]
    for turn, wide_ref in enumerate((mine_ref, other_ref)):
        at = core if turn == 0 else 1 - core
        for which in range(2):
            total = nt_dot(own, wide_ref[1, which]) + nt_dot(own, wide_ref[0, which])
            if which == 1:
                total += own_ref[:, at_block(at, span)].astype(jnp.float32)
            sums_ref[turn, which] = total


def outer_kernel(
    place_ref, sums_ref, all_ref, left_ref, right_ref, mine_ref, other_ref,
    prods_ref, keep_h_ref, send_h_ref, keep_m_ref, *refs,
):
    *send_m_refs, trace_ref, gram_ref = refs
    core, side, line = place_ref[1], place_ref[2], place_ref[3]
    rows, span = left_ref.shape
    lines, piece = keep_h_ref.shape[:2]
    first = core == 0
    left, right = left_ref[...], right_ref[...]
    grams = [None, None]
    for turn, wide_ref in enumerate((mine_ref, other_ref)):
        at = core if turn == 0 else 1 - core
        outer = jnp.where(first, left, right) if turn == 0 else jnp.where(first, right, left)
        columns = at_block(at, span)
        for which in range(2):
            total = sums_ref[turn, which] + nt_dot(outer, wide_ref[1, which]) + nt_dot(outer, wide_ref[0, which])
            prod = total.astype(jnp.bfloat16)
            prods_ref[which, :, columns] = prod
            part = nt_dot(prod, all_ref[:, columns])
            grams[which] = part if grams[which] is None else grams[which] + part
    row = lax.broadcasted_iota(jnp.int32, (rows, 2 * rows), 0)
    col = lax.broadcasted_iota(jnp.int32, (rows, 2 * rows), 1)
    hit = col == row + (row // piece + core) * piece
    trace_ref[...] = jnp.zeros_like(trace_ref)
    for which in range(2):
        trace_ref[which : which + 1, :] = jnp.sum(jnp.where(hit, grams[which], 0.0), axis=0, keepdims=True)
        gram_ref[which] = grams[which]
    for at in range(lines):
        keep_h_ref[at] = gram_ref[0, at_block(2 * at + side, piece), :]
        send_h_ref[at] = gram_ref[0, at_block(2 * at + 1 - side, piece), :].astype(jnp.bfloat16)
    keep_m_ref[...] = gram_ref[1, at_block(line, 2 * piece), :]
    for step, send_ref in enumerate(send_m_refs, 1):
        send_ref[...] = gram_ref[1, at_block(line ^ step, 2 * piece), :].astype(jnp.bfloat16)


def sum_side_kernel(place_ref, keep_ref, got_ref, trace_ref, got_trace_ref, next_ref, next_trace_ref, *send_refs):
    line = place_ref[3]
    next_ref[...] = keep_ref[line] + got_ref[line].astype(jnp.float32)
    for step, send_ref in enumerate(send_refs, 1):
        at = line ^ step
        send_ref[...] = (keep_ref[at] + got_ref[at].astype(jnp.float32)).astype(jnp.bfloat16)
    next_trace_ref[...] = trace_ref[...] + got_trace_ref[...]


def sum_lines_kernel(place_ref, keep_ref, *refs):
    *got_refs, next_ref, send_ref, total_ref = refs
    side = place_ref[2]
    total = keep_ref[...]
    for got_ref in got_refs:
        total += got_ref[...].astype(jnp.float32)
    total_ref[...] = total
    piece = next_ref.shape[0]
    next_ref[...] = total_ref[at_block(side, piece), :]
    send_ref[...] = total_ref[at_block(1 - side, piece), :].astype(jnp.bfloat16)


def last_ham_kernel(place_ref, keep_ref, trace_ref, got_trace_ref, *refs):
    *got_refs, out_ref, next_trace_ref = refs
    total = keep_ref[...]
    for got_ref in got_refs:
        total += got_ref[...].astype(jnp.float32)
    out_ref[...] = total.astype(jnp.bfloat16)
    next_trace_ref[...] = trace_ref[...] + got_trace_ref[...]


def last_metric_kernel(place_ref, keep_ref, got_ref, out_ref):
    out_ref[...] = (keep_ref[...] + got_ref[...].astype(jnp.float32)).astype(jnp.bfloat16)


def interleave(all_ref, mine_ref, cross_ref, core, piece):
    for chip in range(mine_ref.shape[1] // piece):
        source = pl.ds(chip * piece, piece)
        for which in range(2):
            all_ref[which, at_block(2 * chip + core, piece), :] = mine_ref[which, source, :]
            all_ref[which, at_block(2 * chip + 1 - core, piece), :] = cross_ref[which, source, :]


def chip_gradient_kernel(factor, lines, place_ref, prods_ref, cross_ref, far_ref, *refs):
    near_refs, pair_refs, refs = refs[:lines], refs[lines : 2 * lines], refs[2 * lines :]
    *out_refs, bands_ref, all_ref, grad_ref = refs
    chip, core, side, line = place_ref[0], place_ref[1], place_ref[2], place_ref[3]
    piece = near_refs[0].shape[0]
    interleave(all_ref, prods_ref, cross_ref, core, piece)
    for step in range(lines):
        near = at_block(2 * (line ^ step) + side, piece)
        far = at_block(2 * (line ^ step) + 1 - side, piece)
        bands_ref[0, near, :] = near_refs[step][...]
        bands_ref[0, far, :] = far_ref[pl.ds(step * piece, piece), :]
        bands_ref[1, near, :] = pair_refs[step][:piece, :]
        bands_ref[1, far, :] = pair_refs[step][piece:, :]
    total = jnp.dot(bands_ref[0], all_ref[1], preferred_element_type=jnp.float32)
    total += jnp.dot(bands_ref[1], all_ref[0], preferred_element_type=jnp.float32)
    grad_ref[...] = (factor * (4.0 * prods_ref[0].astype(jnp.float32) - 2.0 * total)).astype(jnp.bfloat16)
    for step, out_ref in enumerate(out_refs):
        out_ref[...] = grad_ref[at_block(chip ^ step, piece), :]


def finish_kernel(factor, piece, place_ref, mine_ref, cross_ref, trace_ref, out_ref, energy_ref, all_ref):
    bands = out_ref.shape[0]
    interleave(all_ref, mine_ref, cross_ref, place_ref[1], piece)
    ham, metric = all_ref[0], all_ref[1]
    out_ref[...] = factor * ham.astype(jnp.float32)
    row = lax.broadcasted_iota(jnp.int32, (bands, bands), 0)
    eye = row == lax.broadcasted_iota(jnp.int32, (bands, bands), 1)

    def diagonal(matrix):
        return jnp.sum(jnp.where(eye, matrix.astype(jnp.float32), 0.0), axis=0, keepdims=True)

    exact = trace_ref[...].astype(jnp.bfloat16).astype(jnp.float32)
    ham_exact, metric_exact = exact[0:1, :], exact[1:2, :]
    both = diagonal(jnp.dot(metric, ham, preferred_element_type=jnp.float32))
    both += metric_exact * ham_exact - diagonal(metric) * diagonal(ham)
    energy_ref[0, 0] = factor * jnp.sum(2.0 * ham_exact - both)


def by_chip(coeffs, ham_blocks, metric_blocks, block_cols, block_counts):
    devices = lax.axis_size("rows")
    index = lax.axis_index("rows")
    bands_dev, orbitals = coeffs.shape
    block_rows, slots, size, _ = ham_blocks.shape
    span = block_rows * size
    chips, lines, piece = devices // 2, devices // 4, bands_dev
    rows, bands, width = chips * piece, devices * piece, 2 * span
    chip = index // 2
    place = jnp.stack([chip, index % 2, chip % 2, chip // 2]).astype(jnp.int32)
    bf16, f32 = jnp.bfloat16, jnp.float32

    parts = whole_call(split_kernel, "split", (((piece, width), bf16),) * chips)(place, coeffs)
    cols = block_cols - chip * 2 * block_rows
    cols = jnp.where(cols < 0, cols + 3 * block_rows, cols)
    cols = jnp.where(jnp.arange(slots, dtype=jnp.int32)[None, :] < block_counts[:, None], cols, -1)
    got = [swap(parts[step], 2 * step) for step in range(chips - 1, 0, -1)][::-1]
    mine_in, mine_out, packed = expand_call(tie(cols, parts[0]), ham_blocks, metric_blocks)
    own, low, high = whole_call(
        stack_kernel, "stack", (((rows, width), bf16), ((rows, span), bf16), ((rows, span), bf16))
    )(place, tie(parts[0], mine_in), *got)
    left = lax.ppermute(high, "rows", [(i, i + 2) for i in range(devices - 2)])
    right = lax.ppermute(low, "rows", [(i + 2, i) for i in range(devices - 2)])
    other_in, other_out = expand_call(swap(cols, 1), swap(tie(packed, own), 1))

    every, sums = whole_call(
        functools.partial(inner_kernel, piece),
        "inner",
        (((bands, width), bf16), ((2, 2, rows, span), f32)),
        limit=32,
    )(place, own, swap(own, 1), mine_in, other_in)
    prods, keep_h, send_h, keep_m, *send_m, trace = whole_call(
        outer_kernel,
        "outer",
        (
            ((2, rows, width), bf16),
            ((lines, piece, bands), f32),
            ((lines, piece, bands), bf16),
            ((2 * piece, bands), f32),
        )
        + (((2 * piece, bands), bf16),) * (lines - 1)
        + (((8, bands), f32),),
        (pltpu.VMEM((2, rows, bands), f32),),
        limit=32,
    )(place, sums, every, left, right, mine_out, other_out)

    steps = range(1, lines)
    got_m = [swap(send, 4 * step) for step, send in zip(steps, send_m)]
    got_h = swap(send_h, 2)
    got_trace = swap(trace, 2)
    prods_cross = swap(prods, 1)
    keep_h, trace, *send_h = whole_call(
        sum_side_kernel,
        "sum_side",
        (((piece, bands), f32), ((8, bands), f32)) + (((piece, bands), bf16),) * (lines - 1),
    )(place, keep_h, got_h, trace, got_trace)
    got_h = [swap(send, 4 * step) for step, send in zip(steps, send_h)]
    keep_m, send_m = whole_call(
        sum_lines_kernel,
        "sum_lines",
        (((piece, bands), f32), ((piece, bands), bf16)),
        (pltpu.VMEM((2 * piece, bands), f32),),
    )(place, keep_m, *got_m)
    got_m = swap(send_m, 2)
    got_trace = swap(trace, 4)
    (metric,) = whole_call(last_metric_kernel, "last_metric", (((piece, bands), bf16),))(place, keep_m, got_m)
    ham, trace = whole_call(
        last_ham_kernel, "last_ham", (((piece, bands), bf16), ((8, bands), f32))
    )(place, keep_h, trace, got_trace, *got_h)
    near = [ham] + [swap(ham, 4 * step) for step in steps]
    pair = jnp.concatenate([metric, swap(metric, 2)])
    bit = 8
    while bit < devices:
        trace = trace + swap(trace, bit)
        bit *= 2
    trace = trace + swap(trace, 1)
    far = swap(jnp.concatenate(near), 2)
    pairs = [pair] + [swap(pair, 4 * step) for step in steps]

    factor = math.sqrt(orbitals)
    *grads, matrices = whole_call(
        functools.partial(chip_gradient_kernel, factor, lines),
        "chip_gradient",
        (((piece, width), bf16),) * chips + (((2, rows, bands), bf16),),
        (pltpu.VMEM((2, bands, width), bf16), pltpu.VMEM((rows, width), bf16)),
        limit=32,
    )(place, tie(prods, trace), prods_cross, far, *near, *pairs)
    grads = [grads[0]] + [swap(grad, 2 * step) for step, grad in enumerate(grads[1:], 1)]
    band_hamiltonian, energy = whole_call(
        functools.partial(finish_kernel, factor, piece),
        "finish",
        (((bands, bands), f32), ((1, 1), f32)),
        (pltpu.VMEM((2, bands, bands), bf16),),
        limit=32,
    )(place, matrices, swap(matrices, 1), trace)
    (gradient,) = whole_call(join_kernel, "join", (((piece, orbitals), bf16),))(
        place, tie(grads[0], energy), *grads[1:]
    )
    return (gradient, band_hamiltonian, energy.reshape(1))


def by_device(coeffs, ham_blocks, metric_blocks, block_cols, block_counts):
    devices = lax.axis_size("rows")
    index = lax.axis_index("rows")
    bands_dev, orbitals = coeffs.shape
    block_rows, _, size, _ = ham_blocks.shape
    span = block_rows * size
    bands = bands_dev * devices
    wide = expand(block_cols - (index - 1) * block_rows, block_counts, ham_blocks, metric_blocks)
    own = lax.all_to_all(
        coeffs.reshape(bands_dev, devices, span), "rows", split_axis=1, concat_axis=0, tiled=True
    ).reshape(bands, span)
    left = lax.ppermute(own, "rows", [(i, i + 1) for i in range(devices - 1)])
    right = lax.ppermute(own, "rows", [(i + 1, i) for i in range(devices - 1)])
    ham_prod, metric_prod, *grams = product(left, own, right, wide)
    ham_gram, metric_gram = lax.psum(grams, "rows")
    ham_band, metric_band = ham_gram.astype(jnp.bfloat16), metric_gram.astype(jnp.bfloat16)
    factor = math.sqrt(orbitals)
    grad_rows = gradient_of(factor, ham_band, metric_band, ham_prod, metric_prod)
    gradient = lax.all_to_all(
        grad_rows.reshape(devices, bands_dev, span), "rows", split_axis=0, concat_axis=2, tiled=True
    ).reshape(bands_dev, orbitals)
    ham_wide, metric_wide = ham_band.astype(jnp.float32), metric_band.astype(jnp.float32)
    energy = factor * (2.0 * jnp.trace(ham_wide) - jnp.sum(metric_wide * ham_wide.T))
    return (gradient, factor * ham_wide, energy.reshape(1))


def local(coeffs, *operators):
    devices, bands_dev = lax.axis_size("rows"), coeffs.shape[0]
    paired = devices >= 8 and devices & (devices - 1) == 0 and bands_dev % 16 == 0
    return (by_chip if paired else by_device)(coeffs, *operators)


def solution(mesh):
    in_specs = (
        P(("groups", "rows"), None),
        P(("groups", "rows"), None, None, None),
        P(("groups", "rows"), None, None, None),
        P(("groups", "rows"), None),
        P(("groups", "rows")),
    )
    out_specs = (P(("groups", "rows"), None), P("groups", None), P("groups"))
    return jax.shard_map(local, mesh=mesh, in_specs=in_specs, out_specs=out_specs, check_vma=False)
```

time: 249 us -> 139 us (0.56)
  blocking collectives: 108 us -> 0 us
  matrix products: 35.6 us -> 0 us
  starting transfers between devices: 15.8 us -> 50.7 us
  local copies, waits for them, and re-layouts: 36.9 us -> 4.32 us
  Pallas kernels: 0 us -> 30.5 us
  waiting for transfers between devices: 34.3 us -> 51.3 us
  other arithmetic: 11.7 us -> 0.88 us
  loops' own time: 2.6 us -> 0 us
    psum x1 -> x0, blocking collectives: 108 us -> none  [local(): lax.psum((partial_gram(ham_prod), partial_gram(metric_prod)), 'rows')]
    ppermute x2 -> x41, waiting for transfers between devices: 0.01 us -> 51.3 us  [the longest x39 46.5 us: swap(): return lax.ppermute(value, 'rows', [(i, i ^ bit) for i in range(count)])]
    ppermute x2 -> x41, starting transfers between devices: 4.78 us -> 50.7 us  [the longest x39 44.6 us: swap(): return lax.ppermute(value, 'rows', [(i, i ^ bit) for i in range(count)])]
    dot_general x12 -> x0, matrix products: 35.6 us -> none  [the longest x4 15.4 us: apply_rows(): jnp.einsum('jkrc,mjkc->mjr', metric_part, picked, preferred_element_type=...]
    all_to_all x2 -> x0, waiting for transfers between devices: 34.3 us -> none  [the longest x1 19.5 us: local(): lax.all_to_all(band_rows, 'rows', split_axis=1, concat_axis=0, tiled=True)]
    pallas_call x0 -> x13, Pallas kernels: none -> 30.5 us  [the longest x11 19.6 us: call(): pl.pallas_call(kernel, out_shape=tuple((jax.ShapeDtypeStruct(shape, dtype...]
    convert_element_type x3 -> x0, local copies, waits for them, and re-layouts: 11.1 us -> none  [the longest x2 8.82 us: local(): own_rows.astype(jnp.float32) + metric_full]
    all_to_all x2 -> x0, starting transfers between devices: 11.1 us -> none  [the longest x1 6.61 us: local(): lax.all_to_all(band_rows, 'rows', split_axis=1, concat_axis=0, tiled=True)]
  transfers between devices with their start and end apart: 4 -> 41, of which waited for: 2 -> 16; matrix products, arithmetic and copies ran while one was open for 9% -> 1% of each run, Pallas kernels for 0% -> 15%
where the time goes in v1:
time: 139 us
  waiting for transfers between devices  51.3 us (37%)
  starting transfers between devices  50.7 us (36%)
  Pallas kernels  30.5 us (22%)
  local copies, waits for them, and re-layouts  4.32 us (3%)
    ppermute x39, waiting for transfers between devices, swap(): return lax.ppermute(value, 'rows', [(i, i ^ bit) for i in range(count)])  46.5 us
    ppermute x39, starting transfers between devices, swap(): return lax.ppermute(value, 'rows', [(i, i ^ bit) for i in range(count)])  44.6 us
    pallas_call x11, Pallas kernels, call(): pl.pallas_call(kernel, out_shape=tuple((jax.ShapeDtypeStruct(shape, dtype...  19.6 us
    pallas_call x2, Pallas kernels, expand_call(): pl.pallas_call(expand_own_kernel if own else expand_packed_kernel, out_sh...  10.9 us
    unnamed x6, local copies, waits for them, and re-layouts  4.32 us
    ppermute x1, starting transfers between devices, by_chip(): right = lax.ppermute(low, 'rows', [(i + 2, i) for i in range(devices - 2)])  4 us
    ppermute x1, waiting for transfers between devices, by_chip(): right = lax.ppermute(low, 'rows', [(i + 2, i) for i in range(devices - 2)])  3.62 us
  transfers between devices with their start and end apart: 41, of which 16 were waited for; matrix products, arithmetic and copies ran while one was open for 1% of the time, Pallas kernels for 15%

profile of v1, /device:TPU:9, one launch (start us, length us, event | category | flops | bytes accessed | tf_op | source)
XLA Modules:
  0.0 138.7 jit_solution(15410639650003148175)
XLA Ops:
  0.8 1.1 copy-done.2
  1.9 0.6 split.1
  2.5 1.3 collective-permute-start
  4.0 1.2 collective-permute-start.2
  5.2 2.3 %collective-permute-start.3 = (bf16[48,1024]{1,0:T(8,128)(2,1)S(1)}, bf16[48,1024]{1,0:T(8,128)(2,1)S(1)}, u32[]{:S(2)}, u32[]{:S(2)}) collective-permute-start(bf16[48,1024]{1,0:T(8,128)(2,1)S(1)} %get-tuple-element.61), channel_id=1, source_target_pairs={{0,8},{1,9},{2,10},{3,11},{4,12},{5,13},{6,14},{7,15},{8,0},{9,1},... | collective-permute-start | bytes 294920 | tf_op jit(solution)/shard_map/ppermute | solution.py:136
  7.5 1.0 collective-permute-start.4
  8.5 1.3 collective-permute-start.5
  10.0 0.8 fusion.cols_ref
  10.7 1.6 %copy-done = bf16[8,16,64,64]{3,2,1,0:T(8,128)(2,1)S(1)} copy-done((bf16[8,16,64,64]{3,2,1,0:T(8,128)(2,1)S(1)}, bf16[8,16,64,64]{3,2,1,0:T(8,128)(2,1)}, u32[]{:S(2)}) %copy-start) | copy-done | bytes 1048600
  12.3 1.6 %copy-done.1 = bf16[8,16,64,64]{3,2,1,0:T(8,128)(2,1)S(1)} copy-done((bf16[8,16,64,64]{3,2,1,0:T(8,128)(2,1)S(1)}, bf16[8,16,64,64]{3,2,1,0:T(8,128)(2,1)}, u32[]{:S(2)}) %copy-start.1) | copy-done | bytes 1048600
  13.9 5.7 %expand_own.1 = (bf16[2,2,512,1024]{3,2,1,0:T(8,128)(2,1)S(1)}, bf16[2,2,512,512]{3,2,1,0:T(8,128)(2,1)S(1)}, bf16[2,8,8,64,128]{4,3,2,1,0:T(8,128)(2,1)S(1)}) custom-call(s32[8,16]{1,0:T(8,128)S(1)} %fusion.cols_ref, bf16[8,16,64,64]{3,2,1,0:T(8,128)(2,1)S(1)} %copy-done, bf16[8,16,64,64]{3,2,1,0:T(8,128)(2,1)S(1)} %copy-done.1), custom_call_target="tpu_custom_call" | custom-call | bytes 1024 | tf_op jit(solution)/shard_map/expand_own/pallas_call | solution.py:194
  19.6 2.4 %collective-permute-done.5.refs_6_ = bf16[48,1024]{1,0:T(8,128)(2,1)S(1)} collective-permute-done((bf16[48,1024]{1,0:T(8,128)(2,1)S(1)}, bf16[48,1024]{1,0:T(8,128)(2,1)S(1)}, u32[]{:S(2)}, u32[]{:S(2)}) %collective-permute-start.5) | collective-permute-done | bytes 98336 | tf_op jit(solution)/shard_map/ppermute | solution.py:136
  22.0 3.7 %collective-permute-done.6.refs_7_ = bf16[48,1024]{1,0:T(8,128)(2,1)S(1)} collective-permute-done((bf16[48,1024]{1,0:T(8,128)(2,1)S(1)}, bf16[48,1024]{1,0:T(8,128)(2,1)S(1)}, u32[]{:S(2)}, u32[]{:S(2)}) %collective-permute-start.6) | collective-permute-done | bytes 98336 | tf_op jit(solution)/shard_map/ppermute | solution.py:136
  25.7 0.6 stack.21
  26.4 1.2 collective-permute-start.9
  27.7 2.2 %collective-permute-start.10 = (bf16[384,512]{1,0:T(8,128)(2,1)S(1)}, bf16[384,512]{1,0:T(8,128)(2,1)S(1)}, u32[]{:S(2)}, u32[]{:S(2)}) collective-permute-start(bf16[384,512]{1,0:T(8,128)(2,1)S(1)} %get-tuple-element.71), channel_id=1, source_target_pairs={{0,2},{1,3},{2,4},{3,5},{4,6},{5,7},{6,8},{7,9},{8,10},{9,11},{10,... | collective-permute-start | bytes 1179656 | tf_op jit(solution)/shard_map/ppermute | solution.py:423
  29.9 4.0 %collective-permute-start.11 = (bf16[384,512]{1,0:T(8,128)(2,1)S(1)}, bf16[384,512]{1,0:T(8,128)(2,1)S(1)}, u32[]{:S(2)}, u32[]{:S(2)}) collective-permute-start(bf16[384,512]{1,0:T(8,128)(2,1)S(1)} %get-tuple-element.72), channel_id=1, source_target_pairs={{2,0},{3,1},{4,2},{5,3},{6,4},{7,5},{8,6},{9,7},{10,8},{11,9},{12,... | collective-permute-start | bytes 1179656 | tf_op jit(solution)/shard_map/ppermute | solution.py:424
  33.9 1.1 collective-permute-start.8
  35.0 0.8 collective-permute-done.8.cols_ref
  35.8 5.3 %expand_packed.1 = (bf16[2,2,512,1024]{3,2,1,0:T(8,128)(2,1)S(1)}, bf16[2,2,512,512]{3,2,1,0:T(8,128)(2,1)S(1)}) custom-call(s32[8,16]{1,0:T(8,128)S(1)} %collective-permute-done.8.cols_ref, bf16[2,8,8,64,128]{4,3,2,1,0:T(8,128)(2,1)S(1)} %collective-permute-done.9.packed_ref), custom_call_target="tpu_custom_call" | custom-call | bytes 1024 | tf_op jit(solution)/shard_map/expand_packed/pallas_call | solution.py:194
  41.1 4.1 %inner.1 = (bf16[768,1024]{1,0:T(8,128)(2,1)S(1)}, f32[2,2,384,512]{3,2,1,0:T(8,128)S(1)}) custom-call(s32[4]{0:T(128)S(1)} %pad_add_fusion.place_ref, bf16[384,1024]{1,0:T(8,128)(2,1)S(1)} %get-tuple-element.65.own_ref, bf16[384,1024]{1,0:T(8,128)(2,1)S(1)} %collective-permute-done.7.cross_ref, bf16[2,2,512,1024]{3,2,1,0:T(8,128)(2,1)S(1)} %get-tuple-element.56.mine_ref, ...), custom_call_target="tpu_custom_call" | custom-call | bytes 1024 | tf_op jit(solution)/shard_map/inner/pallas_call | solution.py:230
  45.2 1.1 collective-permute-done.10.left_ref
  46.4 3.6 %collective-permute-done.11.right_ref = bf16[384,512]{1,0:T(8,128)(2,1)S(1)} collective-permute-done((bf16[384,512]{1,0:T(8,128)(2,1)S(1)}, bf16[384,512]{1,0:T(8,128)(2,1)S(1)}, u32[]{:S(2)}, u32[]{:S(2)}) %collective-permute-start.11) | collective-permute-done | bytes 393248 | tf_op jit(solution)/shard_map/ppermute | solution.py:424
  50.0 4.9 %outer.1 = (bf16[2,384,1024]{2,1,0:T(8,128)(2,1)S(1)}, f32[4,48,768]{2,1,0:T(8,128)S(1)}, bf16[4,48,768]{2,1,0:T(8,128)(2,1)S(1)}, f32[96,768]{1,0:T(8,128)S(1)}...) custom-call(s32[4]{0:T(128)S(1)} %pad_add_fusion.place_ref, ...), custom_call_target="tpu_custom_call" | custom-call | bytes 1024 | tf_op jit(solution)/shard_map/outer/pallas_call | solution.py:230
  54.9 0.5 collective-permute-start.20
  55.5 2.7 %collective-permute-start.26 = (bf16[96,768]{1,0:T(8,128)(2,1)S(1)}, bf16[96,768]{1,0:T(8,128)(2,1)S(1)}, u32[]{:S(2)}, u32[]{:S(2)}) collective-permute-start(bf16[96,768]{1,0:T(8,128)(2,1)S(1)} %get-tuple-element.89), channel_id=1, source_target_pairs={{0,8},{1,9},{2,10},{3,11},{4,12},{5,13},{6,14},{7,15},{8,0},{9,1},... | collective-permute-start | bytes 442376 | tf_op jit(solution)/shard_map/ppermute | solution.py:136
  58.1 1.5 %collective-permute-start.13 = (f32[8,768]{1,0:T(8,128)S(1)}, f32[8,768]{1,0:T(8,128)S(1)}, u32[]{:S(2)}, u32[]{:S(2)}) collective-permute-start(f32[8,768]{1,0:T(8,128)S(1)} %get-tuple-element.78.trace_ref), channel_id=1, source_target_pairs={{0,2},{1,3},{2,0},{3,1},{4,6},{5,7},{6,4},{7,5},{8,10},{9,11},{10,... | collective-permute-start | bytes 73736 | tf_op jit(solution)/shard_map/ppermute | solution.py:136
  59.6 5.0 %collective-permute-done.13.got_trace_ref = f32[8,768]{1,0:T(8,128)S(1)} collective-permute-done((f32[8,768]{1,0:T(8,128)S(1)}, f32[8,768]{1,0:T(8,128)S(1)}, u32[]{:S(2)}, u32[]{:S(2)}) %collective-permute-start.13) | collective-permute-done | bytes 24608 | tf_op jit(solution)/shard_map/ppermute | solution.py:136
  64.6 1.5 %collective-permute-start.27 = (bf16[96,768]{1,0:T(8,128)(2,1)S(1)}, bf16[96,768]{1,0:T(8,128)(2,1)S(1)}, u32[]{:S(2)}, u32[]{:S(2)}) collective-permute-start(bf16[96,768]{1,0:T(8,128)(2,1)S(1)} %get-tuple-element.90), channel_id=1, source_target_pairs={{0,12},{1,13},{2,14},{3,15},{4,8},{5,9},{6,10},{7,11},{8,4},{9,5},... | collective-permute-start | bytes 442376 | tf_op jit(solution)/shard_map/ppermute | solution.py:136
  66.1 0.6 sum_side.1
  66.8 1.2 collective-permute-start.16
  67.9 1.5 %collective-permute-start.17 = (bf16[48,768]{1,0:T(8,128)(2,1)S(1)}, bf16[48,768]{1,0:T(8,128)(2,1)S(1)}, u32[]{:S(2)}, u32[]{:S(2)}) collective-permute-start(bf16[48,768]{1,0:T(8,128)(2,1)S(1)} %get-tuple-element.83), channel_id=1, source_target_pairs={{0,12},{1,13},{2,14},{3,15},{4,8},{5,9},{6,10},{7,11},{8,4},{9,5},... | collective-permute-start | bytes 221192 | tf_op jit(solution)/shard_map/ppermute | solution.py:136
  69.4 6.2 %collective-permute-done.27.refs_2_ = bf16[96,768]{1,0:T(8,128)(2,1)S(1)} collective-permute-done((bf16[96,768]{1,0:T(8,128)(2,1)S(1)}, bf16[96,768]{1,0:T(8,128)(2,1)S(1)}, u32[]{:S(2)}, u32[]{:S(2)}) %collective-permute-start.27) | collective-permute-done | bytes 147488 | tf_op jit(solution)/shard_map/ppermute | solution.py:136
  75.7 0.6 sum_lines.1
  76.3 2.3 %collective-permute-done.14.got_trace_ref = f32[8,768]{1,0:T(8,128)S(1)} collective-permute-done((f32[8,768]{1,0:T(8,128)S(1)}, f32[8,768]{1,0:T(8,128)S(1)}, u32[]{:S(2)}, u32[]{:S(2)}) %collective-permute-start.14) | collective-permute-done | bytes 24608 | tf_op jit(solution)/shard_map/ppermute | solution.py:136
  78.6 1.0 collective-permute-start.28
  79.6 0.6 last_ham.1
  80.2 1.5 %collective-permute-start.23 = (bf16[48,768]{1,0:T(8,128)(2,1)S(1)}, bf16[48,768]{1,0:T(8,128)(2,1)S(1)}, u32[]{:S(2)}, u32[]{:S(2)}) collective-permute-start(bf16[48,768]{1,0:T(8,128)(2,1)S(1)} %get-tuple-element.86.refs_0_), channel_id=1, source_target_pairs={{0,12},{1,13},{2,14},{3,15},{4,8},{5,9},{6,10},{7,11},{8,4},{9,5},... | collective-permute-start | bytes 221192 | tf_op jit(solution)/shard_map/ppermute | solution.py:136
  81.7 0.6 collective-permute-start.22
  82.3 0.7 collective-permute-start.21
  82.9 0.6 last_metric.1
  83.5 1.4 collective-permute-start.29
  84.8 2.9 %collective-permute-done.22.refs_2_ = bf16[48,768]{1,0:T(8,128)(2,1)S(1)} collective-permute-done((bf16[48,768]{1,0:T(8,128)(2,1)S(1)}, bf16[48,768]{1,0:T(8,128)(2,1)S(1)}, u32[]{:S(2)}, u32[]{:S(2)}) %collective-permute-start.22) | collective-permute-done | bytes 73760 | tf_op jit(solution)/shard_map/ppermute | solution.py:136
  87.8 1.4 collective-permute-start.24
  89.1 3.1 %collective-permute-start.18 = (f32[8,768]{1,0:T(8,128)S(1)}, f32[8,768]{1,0:T(8,128)S(1)}, u32[]{:S(2)}, u32[]{:S(2)}) collective-permute-start(f32[8,768]{1,0:T(8,128)S(1)} %get-tuple-element.84), channel_id=1, source_target_pairs={{0,8},{1,9},{2,10},{3,11},{4,12},{5,13},{6,14},{7,15},{8,0},{9,1},... | collective-permute-start | bytes 73736 | tf_op jit(solution)/shard_map/ppermute | solution.py:136
  92.2 1.2 collective-permute-done.18
  93.4 2.3 %collective-permute-start.19 = (f32[8,768]{1,0:T(8,128)S(1)}, f32[8,768]{1,0:T(8,128)S(1)}, u32[]{:S(2)}, u32[]{:S(2)}) collective-permute-start(f32[8,768]{1,0:T(8,128)S(1)} %add.25), channel_id=1, source_target_pairs={{0,1},{1,0},{2,3},{3,2},{4,5},{5,4},{6,7},{7,6},{8,9},{9,8},{10,11... | collective-permute-start | bytes 73736 | tf_op jit(solution)/shard_map/ppermute | solution.py:136
  95.8 1.0 collective-permute-start.32
  96.7 2.8 %collective-permute-start.31 = (bf16[96,768]{1,0:T(8,128)(2,1)S(1)}, bf16[96,768]{1,0:T(8,128)(2,1)S(1)}, u32[]{:S(2)}, u32[]{:S(2)}) collective-permute-start(bf16[96,768]{1,0:T(8,128)(2,1)S(1)} %pad_maximum_fusion.1.refs_4_), channel_id=1, source_target_pairs={{0,8},{1,9},{2,10},{3,11},{4,12},{5,13},{6,14},{7,15},{8,0},{9,1},... | collective-permute-start | bytes 442376 | tf_op jit(solution)/shard_map/ppermute | solution.py:136
  99.7 7.9 %collective-permute-done.32.refs_7_ = bf16[96,768]{1,0:T(8,128)(2,1)S(1)} collective-permute-done((bf16[96,768]{1,0:T(8,128)(2,1)S(1)}, bf16[96,768]{1,0:T(8,128)(2,1)S(1)}, u32[]{:S(2)}, u32[]{:S(2)}) %collective-permute-start.32) | collective-permute-done | bytes 147488 | tf_op jit(solution)/shard_map/ppermute | solution.py:136
  107.6 1.9 %collective-permute-done.31.refs_6_ = bf16[96,768]{1,0:T(8,128)(2,1)S(1)} collective-permute-done((bf16[96,768]{1,0:T(8,128)(2,1)S(1)}, bf16[96,768]{1,0:T(8,128)(2,1)S(1)}, u32[]{:S(2)}, u32[]{:S(2)}) %collective-permute-start.31) | collective-permute-done | bytes 147488 | tf_op jit(solution)/shard_map/ppermute | solution.py:136
  109.5 0.6 collective-permute-done.30.refs_5_
  110.1 2.3 %chip_gradient.1 = (bf16[48,1024]{1,0:T(8,128)(2,1)S(1)}, bf16[48,1024]{1,0:T(8,128)(2,1)S(1)}, bf16[48,1024]{1,0:T(8,128)(2,1)S(1)}, bf16[48,1024]{1,0:T(8,128)...) custom-call(s32[4]{0:T(128)S(1)} %pad_add_fusion.place_ref, ...), custom_call_target="tpu_custom_call" | custom-call | bytes 1024 | tf_op jit(solution)/shard_map/chip_gradient/pallas_call | solution.py:230
  112.3 0.9 collective-permute-start.33
  113.4 1.9 %collective-permute-start.35 = (bf16[48,1024]{1,0:T(8,128)(2,1)S(1)}, bf16[48,1024]{1,0:T(8,128)(2,1)S(1)}, u32[]{:S(2)}, u32[]{:S(2)}) collective-permute-start(bf16[48,1024]{1,0:T(8,128)(2,1)S(1)} %get-tuple-element.98), channel_id=1, source_target_pairs={{0,4},{1,5},{2,6},{3,7},{4,0},{5,1},{6,2},{7,3},{8,12},{9,13},{10,... | collective-permute-start | bytes 294920 | tf_op jit(solution)/shard_map/ppermute | solution.py:136
  115.3 1.0 collective-permute-start.36
  116.3 2.1 %collective-permute-start.37 = (bf16[48,1024]{1,0:T(8,128)(2,1)S(1)}, bf16[48,1024]{1,0:T(8,128)(2,1)S(1)}, u32[]{:S(2)}, u32[]{:S(2)}) collective-permute-start(bf16[48,1024]{1,0:T(8,128)(2,1)S(1)} %get-tuple-element.100), channel_id=1, source_target_pairs={{0,8},{1,9},{2,10},{3,11},{4,12},{5,13},{6,14},{7,15},{8,0},{9,1},... | collective-permute-start | bytes 294920 | tf_op jit(solution)/shard_map/ppermute | solution.py:136
  118.4 1.6 %collective-permute-start.38 = (bf16[48,1024]{1,0:T(8,128)(2,1)S(1)}, bf16[48,1024]{1,0:T(8,128)(2,1)S(1)}, u32[]{:S(2)}, u32[]{:S(2)}) collective-permute-start(bf16[48,1024]{1,0:T(8,128)(2,1)S(1)} %get-tuple-element.101), channel_id=1, source_target_pairs={{0,10},{1,11},{2,8},{3,9},{4,14},{5,15},{6,12},{7,13},{8,2},{9,3},... | collective-permute-start | bytes 294920 | tf_op jit(solution)/shard_map/ppermute | solution.py:136
  120.6 1.9 %collective-permute-start.40 = (bf16[48,1024]{1,0:T(8,128)(2,1)S(1)}, bf16[48,1024]{1,0:T(8,128)(2,1)S(1)}, u32[]{:S(2)}, u32[]{:S(2)}) collective-permute-start(bf16[48,1024]{1,0:T(8,128)(2,1)S(1)} %get-tuple-element.103), channel_id=1, source_target_pairs={{0,14},{1,15},{2,12},{3,13},{4,10},{5,11},{6,8},{7,9},{8,6},{9,7},... | collective-permute-start | bytes 294920 | tf_op jit(solution)/shard_map/ppermute | solution.py:136
  122.5 3.2 %finish.1 = (f32[768,768]{1,0:T(8,128)}, f32[1,1]{1,0:T(1,128)}) custom-call(s32[4]{0:T(128)S(1)} %pad_add_fusion.place_ref, bf16[2,384,768]{2,1,0:T(8,128)(2,1)S(1)} %get-tuple-element.94.mine_ref, bf16[2,384,768]{2,1,0:T(8,128)(2,1)S(1)} %collective-permute-done.33.cross_ref, f32[8,768]{1,0:T(8,128)S(1)} %add.26.trace_ref), custom_call_target="tpu_custom_call" | custom-call | bytes 1024 | tf_op jit(solution)/shard_map/finish/pallas_call | solution.py:230
  125.7 5.1 %collective-permute-done.38.refs_5_ = bf16[48,1024]{1,0:T(8,128)(2,1)S(1)} collective-permute-done((bf16[48,1024]{1,0:T(8,128)(2,1)S(1)}, bf16[48,1024]{1,0:T(8,128)(2,1)S(1)}, u32[]{:S(2)}, u32[]{:S(2)}) %collective-permute-start.38) | collective-permute-done | bytes 98336 | tf_op jit(solution)/shard_map/ppermute | solution.py:136
  130.8 3.2 %collective-permute-done.39.refs_6_ = bf16[48,1024]{1,0:T(8,128)(2,1)S(1)} collective-permute-done((bf16[48,1024]{1,0:T(8,128)(2,1)S(1)}, bf16[48,1024]{1,0:T(8,128)(2,1)S(1)}, u32[]{:S(2)}, u32[]{:S(2)}) %collective-permute-start.39) | collective-permute-done | bytes 98336 | tf_op jit(solution)/shard_map/ppermute | solution.py:136
  134.0 3.2 %collective-permute-done.40.refs_7_ = bf16[48,1024]{1,0:T(8,128)(2,1)S(1)} collective-permute-done((bf16[48,1024]{1,0:T(8,128)(2,1)S(1)}, bf16[48,1024]{1,0:T(8,128)(2,1)S(1)}, u32[]{:S(2)}, u32[]{:S(2)}) %collective-permute-start.40) | collective-permute-done | bytes 98336 | tf_op jit(solution)/shard_map/ppermute | solution.py:136
  137.2 1.5 %join.1 = bf16[48,8192]{1,0:T(8,128)(2,1)} custom-call(s32[4]{0:T(128)S(1)} %pad_add_fusion.place_ref, bf16[48,1024]{1,0:T(8,128)(2,1)S(1)} %get-tuple-element.96.refs_0_, bf16[48,1024]{1,0:T(8,128)(2,1)S(1)} %collective-permute-done.34.refs_1_, bf16[48,1024]{1,0:T(8,128)(2,1)S(1)} %collective-permute-done.35.refs_2_, ...), custom_call_target="tpu_custom_call" | custom-call | bytes 1024 | tf_op jit(solution)/shard_map/join/pallas_call | solution.py:230
  (43 shorter events, 1.5 us)
Async XLA Ops:
  0.8 1.1 copy-start.2
  2.5 6.0 %collective-permute-start = (bf16[48,1024]{1,0:T(8,128)(2,1)S(1)}, bf16[48,1024]{1,0:T(8,128)(2,1)S(1)}, u32[]{:S(2)}, u32[]{:S(2)}) collective-permute-start(bf16[48,1024]{1,0:T(8,128)(2,1)S(1)} %get-tuple-element.58), channel_id=1, source_target_pairs={{0,2},{1,3},{2,0},{3,1},{4,6},{5,7},{6,4},{7,5},{8,10},{9,11},{10,... | collective-permute-start | bytes 294920 | tf_op jit(solution)/shard_map/ppermute | solution.py:136
  3.8 6.0 %collective-permute-start.1 = (bf16[48,1024]{1,0:T(8,128)(2,1)S(1)}, bf16[48,1024]{1,0:T(8,128)(2,1)S(1)}, u32[]{:S(2)}, u32[]{:S(2)}) collective-permute-start(bf16[48,1024]{1,0:T(8,128)(2,1)S(1)} %get-tuple-element.59), channel_id=1, source_target_pairs={{0,4},{1,5},{2,6},{3,7},{4,0},{5,1},{6,2},{7,3},{8,12},{9,13},{10,... | collective-permute-start | bytes 294920 | tf_op jit(solution)/shard_map/ppermute | solution.py:136
  4.0 15.6 %collective-permute-start.2 = (bf16[48,1024]{1,0:T(8,128)(2,1)S(1)}, bf16[48,1024]{1,0:T(8,128)(2,1)S(1)}, u32[]{:S(2)}, u32[]{:S(2)}) collective-permute-start(bf16[48,1024]{1,0:T(8,128)(2,1)S(1)} %get-tuple-element.60), channel_id=1, source_target_pairs={{0,6},{1,7},{2,4},{3,5},{4,2},{5,3},{6,0},{7,1},{8,14},{9,15},{10,... | collective-permute-start | bytes 294920 | tf_op jit(solution)/shard_map/ppermute | solution.py:136
  5.2 14.4 %collective-permute-start.3 = (bf16[48,1024]{1,0:T(8,128)(2,1)S(1)}, bf16[48,1024]{1,0:T(8,128)(2,1)S(1)}, u32[]{:S(2)}, u32[]{:S(2)}) collective-permute-start(bf16[48,1024]{1,0:T(8,128)(2,1)S(1)} %get-tuple-element.61), channel_id=1, source_target_pairs={{0,8},{1,9},{2,10},{3,11},{4,12},{5,13},{6,14},{7,15},{8,0},{9,1},... | collective-permute-start | bytes 294920 | tf_op jit(solution)/shard_map/ppermute | solution.py:136
  7.5 12.1 %collective-permute-start.4 = (bf16[48,1024]{1,0:T(8,128)(2,1)S(1)}, bf16[48,1024]{1,0:T(8,128)(2,1)S(1)}, u32[]{:S(2)}, u32[]{:S(2)}) collective-permute-start(bf16[48,1024]{1,0:T(8,128)(2,1)S(1)} %get-tuple-element.62), channel_id=1, source_target_pairs={{0,10},{1,11},{2,8},{3,9},{4,14},{5,15},{6,12},{7,13},{8,2},{9,3},... | collective-permute-start | bytes 294920 | tf_op jit(solution)/shard_map/ppermute | solution.py:136
  8.5 13.5 %collective-permute-start.5 = (bf16[48,1024]{1,0:T(8,128)(2,1)S(1)}, bf16[48,1024]{1,0:T(8,128)(2,1)S(1)}, u32[]{:S(2)}, u32[]{:S(2)}) collective-permute-start(bf16[48,1024]{1,0:T(8,128)(2,1)S(1)} %get-tuple-element.63), channel_id=1, source_target_pairs={{0,12},{1,13},{2,14},{3,15},{4,8},{5,9},{6,10},{7,11},{8,4},{9,5},... | collective-permute-start | bytes 294920 | tf_op jit(solution)/shard_map/ppermute | solution.py:136
  9.8 15.9 %collective-permute-start.6 = (bf16[48,1024]{1,0:T(8,128)(2,1)S(1)}, bf16[48,1024]{1,0:T(8,128)(2,1)S(1)}, u32[]{:S(2)}, u32[]{:S(2)}) collective-permute-start(bf16[48,1024]{1,0:T(8,128)(2,1)S(1)} %get-tuple-element.64), channel_id=1, source_target_pairs={{0,14},{1,15},{2,12},{3,13},{4,10},{5,11},{6,8},{7,9},{8,6},{9,7},... | collective-permute-start | bytes 294920 | tf_op jit(solution)/shard_map/ppermute | solution.py:136
  10.7 1.6 %copy-start = (bf16[8,16,64,64]{3,2,1,0:T(8,128)(2,1)S(1)}, bf16[8,16,64,64]{3,2,1,0:T(8,128)(2,1)}, u32[]{:S(2)}) copy-start(bf16[8,16,64,64]{3,2,1,0:T(8,128)(2,1)} %ham_ref.1) | copy-start | bytes 3145732
  12.3 1.6 %copy-start.1 = (bf16[8,16,64,64]{3,2,1,0:T(8,128)(2,1)S(1)}, bf16[8,16,64,64]{3,2,1,0:T(8,128)(2,1)}, u32[]{:S(2)}) copy-start(bf16[8,16,64,64]{3,2,1,0:T(8,128)(2,1)} %metric_ref.1) | copy-start | bytes 3145732
  26.4 9.4 %collective-permute-start.9 = (bf16[2,8,8,64,128]{4,3,2,1,0:T(8,128)(2,1)S(1)}, bf16[2,8,8,64,128]{4,3,2,1,0:T(8,128)(2,1)S(1)}, u32[]{:S(2)}, u32[]{:S(2)}) collective-permute-start(bf16[2,8,8,64,128]{4,3,2,1,0:T(8,128)(2,1)S(1)} %get-tuple-element.67), channel_id=1, source_target_pairs={{0,1},{1,0},{2,3},{3,2},{4,5},{5,4},{6,7},{7,6},{8,9},{9,8},{10,11... | collective-permute-start | bytes 6291464 | tf_op jit(solution)/shard_map/ppermute | solution.py:136
  27.6 13.5 %collective-permute-start.7 = (bf16[384,1024]{1,0:T(8,128)(2,1)S(1)}, bf16[384,1024]{1,0:T(8,128)(2,1)S(1)}, u32[]{:S(2)}, u32[]{:S(2)}) collective-permute-start(bf16[384,1024]{1,0:T(8,128)(2,1)S(1)} %get-tuple-element.65.own_ref), channel_id=1, source_target_pairs={{0,1},{1,0},{2,3},{3,2},{4,5},{5,4},{6,7},{7,6},{8,9},{9,8},{10,11... | collective-permute-start | bytes 2359304 | tf_op jit(solution)/shard_map/ppermute | solution.py:136
  27.7 18.6 %collective-permute-start.10 = (bf16[384,512]{1,0:T(8,128)(2,1)S(1)}, bf16[384,512]{1,0:T(8,128)(2,1)S(1)}, u32[]{:S(2)}, u32[]{:S(2)}) collective-permute-start(bf16[384,512]{1,0:T(8,128)(2,1)S(1)} %get-tuple-element.71), channel_id=1, source_target_pairs={{0,2},{1,3},{2,4},{3,5},{4,6},{5,7},{6,8},{7,9},{8,10},{9,11},{10,... | collective-permute-start | bytes 1179656 | tf_op jit(solution)/shard_map/ppermute | solution.py:423
  29.9 20.1 %collective-permute-start.11 = (bf16[384,512]{1,0:T(8,128)(2,1)S(1)}, bf16[384,512]{1,0:T(8,128)(2,1)S(1)}, u32[]{:S(2)}, u32[]{:S(2)}) collective-permute-start(bf16[384,512]{1,0:T(8,128)(2,1)S(1)} %get-tuple-element.72), channel_id=1, source_target_pairs={{2,0},{3,1},{4,2},{5,3},{6,4},{7,5},{8,6},{9,7},{10,8},{11,9},{12,... | collective-permute-start | bytes 1179656 | tf_op jit(solution)/shard_map/ppermute | solution.py:424
  33.9 1.9 %collective-permute-start.8 = (s32[8,16]{1,0:T(8,128)S(1)}, s32[8,16]{1,0:T(8,128)S(1)}, u32[]{:S(2)}, u32[]{:S(2)}) collective-permute-start(s32[8,16]{1,0:T(8,128)S(1)} %fusion.cols_ref), channel_id=1, source_target_pairs={{0,1},{1,0},{2,3},{3,2},{4,5},{5,4},{6,7},{7,6},{8,9},{9,8},{10,11... | collective-permute-start | bytes 1544 | tf_op jit(solution)/shard_map/ppermute | solution.py:136
  54.9 55.1 %collective-permute-start.20 = (bf16[2,384,1024]{2,1,0:T(8,128)(2,1)S(1)}, bf16[2,384,1024]{2,1,0:T(8,128)(2,1)S(1)}, u32[]{:S(2)}, u32[]{:S(2)}) collective-permute-start(bf16[2,384,1024]{2,1,0:T(8,128)(2,1)S(1)} %get-tuple-element.85.prods_ref), channel_id=1, source_target_pairs={{0,1},{1,0},{2,3},{3,2},{4,5},{5,4},{6,7},{7,6},{8,9},{9,8},{10,11... | collective-permute-start | bytes 4718600 | tf_op jit(solution)/shard_map/ppermute | solution.py:136
  55.5 10.6 %collective-permute-start.12 = (bf16[4,48,768]{2,1,0:T(8,128)(2,1)S(1)}, bf16[4,48,768]{2,1,0:T(8,128)(2,1)S(1)}, u32[]{:S(2)}, u32[]{:S(2)}) collective-permute-start(bf16[4,48,768]{2,1,0:T(8,128)(2,1)S(1)} %get-tuple-element.77), channel_id=1, source_target_pairs={{0,2},{1,3},{2,0},{3,1},{4,6},{5,7},{6,4},{7,5},{8,10},{9,11},{10,... | collective-permute-start | bytes 884744 | tf_op jit(solution)/shard_map/ppermute | solution.py:136
  55.5 11.3 %collective-permute-start.25 = (bf16[96,768]{1,0:T(8,128)(2,1)S(1)}, bf16[96,768]{1,0:T(8,128)(2,1)S(1)}, u32[]{:S(2)}, u32[]{:S(2)}) collective-permute-start(bf16[96,768]{1,0:T(8,128)(2,1)S(1)} %get-tuple-element.88), channel_id=1, source_target_pairs={{0,4},{1,5},{2,6},{3,7},{4,0},{5,1},{6,2},{7,3},{8,12},{9,13},{10,... | collective-permute-start | bytes 442376 | tf_op jit(solution)/shard_map/ppermute | solution.py:136
  55.5 12.5 %collective-permute-start.26 = (bf16[96,768]{1,0:T(8,128)(2,1)S(1)}, bf16[96,768]{1,0:T(8,128)(2,1)S(1)}, u32[]{:S(2)}, u32[]{:S(2)}) collective-permute-start(bf16[96,768]{1,0:T(8,128)(2,1)S(1)} %get-tuple-element.89), channel_id=1, source_target_pairs={{0,8},{1,9},{2,10},{3,11},{4,12},{5,13},{6,14},{7,15},{8,0},{9,1},... | collective-permute-start | bytes 442376 | tf_op jit(solution)/shard_map/ppermute | solution.py:136
  58.1 6.5 %collective-permute-start.13 = (f32[8,768]{1,0:T(8,128)S(1)}, f32[8,768]{1,0:T(8,128)S(1)}, u32[]{:S(2)}, u32[]{:S(2)}) collective-permute-start(f32[8,768]{1,0:T(8,128)S(1)} %get-tuple-element.78.trace_ref), channel_id=1, source_target_pairs={{0,2},{1,3},{2,0},{3,1},{4,6},{5,7},{6,4},{7,5},{8,10},{9,11},{10,... | collective-permute-start | bytes 73736 | tf_op jit(solution)/shard_map/ppermute | solution.py:136
  64.6 11.1 %collective-permute-start.27 = (bf16[96,768]{1,0:T(8,128)(2,1)S(1)}, bf16[96,768]{1,0:T(8,128)(2,1)S(1)}, u32[]{:S(2)}, u32[]{:S(2)}) collective-permute-start(bf16[96,768]{1,0:T(8,128)(2,1)S(1)} %get-tuple-element.90), channel_id=1, source_target_pairs={{0,12},{1,13},{2,14},{3,15},{4,8},{5,9},{6,10},{7,11},{8,4},{9,5},... | collective-permute-start | bytes 442376 | tf_op jit(solution)/shard_map/ppermute | solution.py:136
  66.7 12.9 %collective-permute-start.15 = (bf16[48,768]{1,0:T(8,128)(2,1)S(1)}, bf16[48,768]{1,0:T(8,128)(2,1)S(1)}, u32[]{:S(2)}, u32[]{:S(2)}) collective-permute-start(bf16[48,768]{1,0:T(8,128)(2,1)S(1)} %get-tuple-element.81), channel_id=1, source_target_pairs={{0,4},{1,5},{2,6},{3,7},{4,0},{5,1},{6,2},{7,3},{8,12},{9,13},{10,... | collective-permute-start | bytes 221192 | tf_op jit(solution)/shard_map/ppermute | solution.py:136
  66.8 12.8 %collective-permute-start.16 = (bf16[48,768]{1,0:T(8,128)(2,1)S(1)}, bf16[48,768]{1,0:T(8,128)(2,1)S(1)}, u32[]{:S(2)}, u32[]{:S(2)}) collective-permute-start(bf16[48,768]{1,0:T(8,128)(2,1)S(1)} %get-tuple-element.82), channel_id=1, source_target_pairs={{0,8},{1,9},{2,10},{3,11},{4,12},{5,13},{6,14},{7,15},{8,0},{9,1},... | collective-permute-start | bytes 221192 | tf_op jit(solution)/shard_map/ppermute | solution.py:136
  67.9 11.7 %collective-permute-start.17 = (bf16[48,768]{1,0:T(8,128)(2,1)S(1)}, bf16[48,768]{1,0:T(8,128)(2,1)S(1)}, u32[]{:S(2)}, u32[]{:S(2)}) collective-permute-start(bf16[48,768]{1,0:T(8,128)(2,1)S(1)} %get-tuple-element.83), channel_id=1, source_target_pairs={{0,12},{1,13},{2,14},{3,15},{4,8},{5,9},{6,10},{7,11},{8,4},{9,5},... | collective-permute-start | bytes 221192 | tf_op jit(solution)/shard_map/ppermute | solution.py:136
  75.6 3.0 %collective-permute-start.14 = (f32[8,768]{1,0:T(8,128)S(1)}, f32[8,768]{1,0:T(8,128)S(1)}, u32[]{:S(2)}, u32[]{:S(2)}) collective-permute-start(f32[8,768]{1,0:T(8,128)S(1)} %get-tuple-element.80.trace_ref), channel_id=1, source_target_pairs={{0,4},{1,5},{2,6},{3,7},{4,0},{5,1},{6,2},{7,3},{8,12},{9,13},{10,... | collective-permute-start | bytes 73736 | tf_op jit(solution)/shard_map/ppermute | solution.py:136
  78.6 4.3 %collective-permute-start.28 = (bf16[48,768]{1,0:T(8,128)(2,1)S(1)}, bf16[48,768]{1,0:T(8,128)(2,1)S(1)}, u32[]{:S(2)}, u32[]{:S(2)}) collective-permute-start(bf16[48,768]{1,0:T(8,128)(2,1)S(1)} %get-tuple-element.92), channel_id=1, source_target_pairs={{0,2},{1,3},{2,0},{3,1},{4,6},{5,7},{6,4},{7,5},{8,10},{9,11},{10,... | collective-permute-start | bytes 221192 | tf_op jit(solution)/shard_map/ppermute | solution.py:136
  80.2 4.7 %collective-permute-start.23 = (bf16[48,768]{1,0:T(8,128)(2,1)S(1)}, bf16[48,768]{1,0:T(8,128)(2,1)S(1)}, u32[]{:S(2)}, u32[]{:S(2)}) collective-permute-start(bf16[48,768]{1,0:T(8,128)(2,1)S(1)} %get-tuple-element.86.refs_0_), channel_id=1, source_target_pairs={{0,12},{1,13},{2,14},{3,15},{4,8},{5,9},{6,10},{7,11},{8,4},{9,5},... | collective-permute-start | bytes 221192 | tf_op jit(solution)/shard_map/ppermute | solution.py:136
  81.7 6.1 %collective-permute-start.22 = (bf16[48,768]{1,0:T(8,128)(2,1)S(1)}, bf16[48,768]{1,0:T(8,128)(2,1)S(1)}, u32[]{:S(2)}, u32[]{:S(2)}) collective-permute-start(bf16[48,768]{1,0:T(8,128)(2,1)S(1)} %get-tuple-element.86.refs_0_), channel_id=1, source_target_pairs={{0,8},{1,9},{2,10},{3,11},{4,12},{5,13},{6,14},{7,15},{8,0},{9,1},... | collective-permute-start | bytes 221192 | tf_op jit(solution)/shard_map/ppermute | solution.py:136
  82.3 5.5 %collective-permute-start.21 = (bf16[48,768]{1,0:T(8,128)(2,1)S(1)}, bf16[48,768]{1,0:T(8,128)(2,1)S(1)}, u32[]{:S(2)}, u32[]{:S(2)}) collective-permute-start(bf16[48,768]{1,0:T(8,128)(2,1)S(1)} %get-tuple-element.86.refs_0_), channel_id=1, source_target_pairs={{0,4},{1,5},{2,6},{3,7},{4,0},{5,1},{6,2},{7,3},{8,12},{9,13},{10,... | collective-permute-start | bytes 221192 | tf_op jit(solution)/shard_map/ppermute | solution.py:136
  83.5 12.2 %collective-permute-start.29 = (bf16[48,768]{1,0:T(8,128)(2,1)S(1)}, bf16[48,768]{1,0:T(8,128)(2,1)S(1)}, u32[]{:S(2)}, u32[]{:S(2)}) collective-permute-start(bf16[48,768]{1,0:T(8,128)(2,1)S(1)} %last_metric.1), channel_id=1, source_target_pairs={{0,2},{1,3},{2,0},{3,1},{4,6},{5,7},{6,4},{7,5},{8,10},{9,11},{10,... | collective-permute-start | bytes 221192 | tf_op jit(solution)/shard_map/ppermute | solution.py:136
  87.8 22.3 %collective-permute-start.24 = (bf16[192,768]{1,0:T(8,128)(2,1)S(1)}, bf16[192,768]{1,0:T(8,128)(2,1)S(1)}, u32[]{:S(2)}, u32[]{:S(2)}) collective-permute-start(bf16[192,768]{1,0:T(8,128)(2,1)S(1)} %pad_maximum_fusion), channel_id=1, source_target_pairs={{0,2},{1,3},{2,0},{3,1},{4,6},{5,7},{6,4},{7,5},{8,10},{9,11},{10,... | collective-permute-start | bytes 884744 | tf_op jit(solution)/shard_map/ppermute | solution.py:136
  89.1 4.3 %collective-permute-start.18 = (f32[8,768]{1,0:T(8,128)S(1)}, f32[8,768]{1,0:T(8,128)S(1)}, u32[]{:S(2)}, u32[]{:S(2)}) collective-permute-start(f32[8,768]{1,0:T(8,128)S(1)} %get-tuple-element.84), channel_id=1, source_target_pairs={{0,8},{1,9},{2,10},{3,11},{4,12},{5,13},{6,14},{7,15},{8,0},{9,1},... | collective-permute-start | bytes 73736 | tf_op jit(solution)/shard_map/ppermute | solution.py:136
  93.4 6.1 %collective-permute-start.19 = (f32[8,768]{1,0:T(8,128)S(1)}, f32[8,768]{1,0:T(8,128)S(1)}, u32[]{:S(2)}, u32[]{:S(2)}) collective-permute-start(f32[8,768]{1,0:T(8,128)S(1)} %add.25), channel_id=1, source_target_pairs={{0,1},{1,0},{2,3},{3,2},{4,5},{5,4},{6,7},{7,6},{8,9},{9,8},{10,11... | collective-permute-start | bytes 73736 | tf_op jit(solution)/shard_map/ppermute | solution.py:136
  95.8 11.8 %collective-permute-start.32 = (bf16[96,768]{1,0:T(8,128)(2,1)S(1)}, bf16[96,768]{1,0:T(8,128)(2,1)S(1)}, u32[]{:S(2)}, u32[]{:S(2)}) collective-permute-start(bf16[96,768]{1,0:T(8,128)(2,1)S(1)} %pad_maximum_fusion.1.refs_4_), channel_id=1, source_target_pairs={{0,12},{1,13},{2,14},{3,15},{4,8},{5,9},{6,10},{7,11},{8,4},{9,5},... | collective-permute-start | bytes 442376 | tf_op jit(solution)/shard_map/ppermute | solution.py:136
  96.7 12.7 %collective-permute-start.31 = (bf16[96,768]{1,0:T(8,128)(2,1)S(1)}, bf16[96,768]{1,0:T(8,128)(2,1)S(1)}, u32[]{:S(2)}, u32[]{:S(2)}) collective-permute-start(bf16[96,768]{1,0:T(8,128)(2,1)S(1)} %pad_maximum_fusion.1.refs_4_), channel_id=1, source_target_pairs={{0,8},{1,9},{2,10},{3,11},{4,12},{5,13},{6,14},{7,15},{8,0},{9,1},... | collective-permute-start | bytes 442376 | tf_op jit(solution)/shard_map/ppermute | solution.py:136
  99.6 10.5 %collective-permute-start.30 = (bf16[96,768]{1,0:T(8,128)(2,1)S(1)}, bf16[96,768]{1,0:T(8,128)(2,1)S(1)}, u32[]{:S(2)}, u32[]{:S(2)}) collective-permute-start(bf16[96,768]{1,0:T(8,128)(2,1)S(1)} %pad_maximum_fusion.1.refs_4_), channel_id=1, source_target_pairs={{0,4},{1,5},{2,6},{3,7},{4,0},{5,1},{6,2},{7,3},{8,12},{9,13},{10,... | collective-permute-start | bytes 442376 | tf_op jit(solution)/shard_map/ppermute | solution.py:136
  112.3 8.2 %collective-permute-start.33 = (bf16[2,384,768]{2,1,0:T(8,128)(2,1)S(1)}, bf16[2,384,768]{2,1,0:T(8,128)(2,1)S(1)}, u32[]{:S(2)}, u32[]{:S(2)}) collective-permute-start(bf16[2,384,768]{2,1,0:T(8,128)(2,1)S(1)} %get-tuple-element.94.mine_ref), channel_id=1, source_target_pairs={{0,1},{1,0},{2,3},{3,2},{4,5},{5,4},{6,7},{7,6},{8,9},{9,8},{10,11... | collective-permute-start | bytes 3538952 | tf_op jit(solution)/shard_map/ppermute | solution.py:136
  113.2 5.2 %collective-permute-start.34 = (bf16[48,1024]{1,0:T(8,128)(2,1)S(1)}, bf16[48,1024]{1,0:T(8,128)(2,1)S(1)}, u32[]{:S(2)}, u32[]{:S(2)}) collective-permute-start(bf16[48,1024]{1,0:T(8,128)(2,1)S(1)} %get-tuple-element.97), channel_id=1, source_target_pairs={{0,2},{1,3},{2,0},{3,1},{4,6},{5,7},{6,4},{7,5},{8,10},{9,11},{10,... | collective-permute-start | bytes 294920 | tf_op jit(solution)/shard_map/ppermute | solution.py:136
  113.4 6.6 %collective-permute-start.35 = (bf16[48,1024]{1,0:T(8,128)(2,1)S(1)}, bf16[48,1024]{1,0:T(8,128)(2,1)S(1)}, u32[]{:S(2)}, u32[]{:S(2)}) collective-permute-start(bf16[48,1024]{1,0:T(8,128)(2,1)S(1)} %get-tuple-element.98), channel_id=1, source_target_pairs={{0,4},{1,5},{2,6},{3,7},{4,0},{5,1},{6,2},{7,3},{8,12},{9,13},{10,... | collective-permute-start | bytes 294920 | tf_op jit(solution)/shard_map/ppermute | solution.py:136
  115.3 10.4 %collective-permute-start.36 = (bf16[48,1024]{1,0:T(8,128)(2,1)S(1)}, bf16[48,1024]{1,0:T(8,128)(2,1)S(1)}, u32[]{:S(2)}, u32[]{:S(2)}) collective-permute-start(bf16[48,1024]{1,0:T(8,128)(2,1)S(1)} %get-tuple-element.99), channel_id=1, source_target_pairs={{0,6},{1,7},{2,4},{3,5},{4,2},{5,3},{6,0},{7,1},{8,14},{9,15},{10,... | collective-permute-start | bytes 294920 | tf_op jit(solution)/shard_map/ppermute | solution.py:136
  116.3 9.4 %collective-permute-start.37 = (bf16[48,1024]{1,0:T(8,128)(2,1)S(1)}, bf16[48,1024]{1,0:T(8,128)(2,1)S(1)}, u32[]{:S(2)}, u32[]{:S(2)}) collective-permute-start(bf16[48,1024]{1,0:T(8,128)(2,1)S(1)} %get-tuple-element.100), channel_id=1, source_target_pairs={{0,8},{1,9},{2,10},{3,11},{4,12},{5,13},{6,14},{7,15},{8,0},{9,1},... | collective-permute-start | bytes 294920 | tf_op jit(solution)/shard_map/ppermute | solution.py:136
  118.4 12.4 %collective-permute-start.38 = (bf16[48,1024]{1,0:T(8,128)(2,1)S(1)}, bf16[48,1024]{1,0:T(8,128)(2,1)S(1)}, u32[]{:S(2)}, u32[]{:S(2)}) collective-permute-start(bf16[48,1024]{1,0:T(8,128)(2,1)S(1)} %get-tuple-element.101), channel_id=1, source_target_pairs={{0,10},{1,11},{2,8},{3,9},{4,14},{5,15},{6,12},{7,13},{8,2},{9,3},... | collective-permute-start | bytes 294920 | tf_op jit(solution)/shard_map/ppermute | solution.py:136
  120.0 14.0 %collective-permute-start.39 = (bf16[48,1024]{1,0:T(8,128)(2,1)S(1)}, bf16[48,1024]{1,0:T(8,128)(2,1)S(1)}, u32[]{:S(2)}, u32[]{:S(2)}) collective-permute-start(bf16[48,1024]{1,0:T(8,128)(2,1)S(1)} %get-tuple-element.102), channel_id=1, source_target_pairs={{0,12},{1,13},{2,14},{3,15},{4,8},{5,9},{6,10},{7,11},{8,4},{9,5},... | collective-permute-start | bytes 294920 | tf_op jit(solution)/shard_map/ppermute | solution.py:136
  120.6 16.6 %collective-permute-start.40 = (bf16[48,1024]{1,0:T(8,128)(2,1)S(1)}, bf16[48,1024]{1,0:T(8,128)(2,1)S(1)}, u32[]{:S(2)}, u32[]{:S(2)}) collective-permute-start(bf16[48,1024]{1,0:T(8,128)(2,1)S(1)} %get-tuple-element.103), channel_id=1, source_target_pairs={{0,14},{1,15},{2,12},{3,13},{4,10},{5,11},{6,8},{7,9},{8,6},{9,7},... | collective-permute-start | bytes 294920 | tf_op jit(solution)/shard_map/ppermute | solution.py:136

commit v2 on v1

--- a/solution.py
+++ b/solution.py
@@ -340,17 +340,14 @@
     send_ref[...] = total_ref[at_block(1 - side, piece), :].astype(jnp.bfloat16)
 
 
-def last_ham_kernel(place_ref, keep_ref, trace_ref, got_trace_ref, *refs):
+def last_kernel(place_ref, keep_h_ref, keep_m_ref, got_m_ref, trace_ref, got_trace_ref, *refs):
     *got_refs, out_ref, next_trace_ref = refs
-    total = keep_ref[...]
+    total = keep_h_ref[...]
     for got_ref in got_refs:
         total += got_ref[...].astype(jnp.float32)
-    out_ref[...] = total.astype(jnp.bfloat16)
+    out_ref[0] = total.astype(jnp.bfloat16)
+    out_ref[1] = (keep_m_ref[...] + got_m_ref[...].astype(jnp.float32)).astype(jnp.bfloat16)
     next_trace_ref[...] = trace_ref[...] + got_trace_ref[...]
-
-
-def last_metric_kernel(place_ref, keep_ref, got_ref, out_ref):
-    out_ref[...] = (keep_ref[...] + got_ref[...].astype(jnp.float32)).astype(jnp.bfloat16)
 
 
 def interleave(all_ref, mine_ref, cross_ref, core, piece):
@@ -361,24 +358,38 @@
             all_ref[which, at_block(2 * chip + 1 - core, piece), :] = cross_ref[which, source, :]
 
 
-def chip_gradient_kernel(factor, lines, place_ref, prods_ref, cross_ref, far_ref, *refs):
-    near_refs, pair_refs, refs = refs[:lines], refs[lines : 2 * lines], refs[2 * lines :]
-    *out_refs, bands_ref, all_ref, grad_ref = refs
-    chip, core, side, line = place_ref[0], place_ref[1], place_ref[2], place_ref[3]
-    piece = near_refs[0].shape[0]
-    interleave(all_ref, prods_ref, cross_ref, core, piece)
-    for step in range(lines):
-        near = at_block(2 * (line ^ step) + side, piece)
-        far = at_block(2 * (line ^ step) + 1 - side, piece)
-        bands_ref[0, near, :] = near_refs[step][...]
-        bands_ref[0, far, :] = far_ref[pl.ds(step * piece, piece), :]
-        bands_ref[1, near, :] = pair_refs[step][:piece, :]
-        bands_ref[1, far, :] = pair_refs[step][piece:, :]
+def interleave_kernel(piece, place_ref, mine_ref, cross_ref, all_ref):
+    interleave(all_ref, mine_ref, cross_ref, place_ref[1], piece)
+
+
+def chip_gradient_kernel(factor, far, place_ref, prods_ref, all_ref, *refs):
+    count = all_ref.shape[1] // (4 * refs[0].shape[1])
+    piece_refs, refs = refs[:count], refs[count:]
+    piece = piece_refs[0].shape[1]
+    if far:
+        near_refs, (*out_refs, bands_ref) = refs[:count], refs[count:]
+    else:
+        *out_refs, bands_ref = refs
+    side, line = place_ref[2], place_ref[3]
+    if far:
+        side = 1 - side
+
+    def rows_of(step, at):
+        return at_block(2 * (line ^ step) + at, piece)
+
+    if far:
+        matrices_ref = out_refs.pop()
+        for step in range(count):
+            matrices_ref[:, rows_of(step, 1 - side), :] = near_refs[step][...]
+            matrices_ref[:, rows_of(step, side), :] = piece_refs[step][...]
+    for step in range(count):
+        bands_ref[:, pl.ds(step * piece, piece), :] = piece_refs[step][...]
     total = jnp.dot(bands_ref[0], all_ref[1], preferred_element_type=jnp.float32)
     total += jnp.dot(bands_ref[1], all_ref[0], preferred_element_type=jnp.float32)
-    grad_ref[...] = (factor * (4.0 * prods_ref[0].astype(jnp.float32) - 2.0 * total)).astype(jnp.bfloat16)
     for step, out_ref in enumerate(out_refs):
-        out_ref[...] = grad_ref[at_block(chip ^ step, piece), :]
+        part = 4.0 * prods_ref[0, rows_of(step, side), :].astype(jnp.float32)
+        part -= 2.0 * total[step * piece : (step + 1) * piece, :]
+        out_ref[...] = (factor * part).astype(jnp.bfloat16)
 
 
 def finish_kernel(factor, piece, place_ref, mine_ref, cross_ref, trace_ref, out_ref, energy_ref, all_ref):
@@ -449,51 +460,58 @@
     got_m = [swap(send, 4 * step) for step, send in zip(steps, send_m)]
     got_h = swap(send_h, 2)
     got_trace = swap(trace, 2)
-    prods_cross = swap(prods, 1)
     keep_h, trace, *send_h = whole_call(
         sum_side_kernel,
         "sum_side",
         (((piece, bands), f32), ((8, bands), f32)) + (((piece, bands), bf16),) * (lines - 1),
     )(place, keep_h, got_h, trace, got_trace)
-    got_h = [swap(send, 4 * step) for step, send in zip(steps, send_h)]
+    got_h = [swap(tie(send, *got_m), 4 * step) for step, send in zip(steps, send_h)]
+    (prods_all,) = whole_call(
+        functools.partial(interleave_kernel, piece), "interleave", (((2, bands, width), bf16),), limit=16
+    )(place, prods, swap(prods, 1))
     keep_m, send_m = whole_call(
         sum_lines_kernel,
         "sum_lines",
         (((piece, bands), f32), ((piece, bands), bf16)),
         (pltpu.VMEM((2 * piece, bands), f32),),
-    )(place, keep_m, *got_m)
+    )(place, tie(keep_m, prods_all), *got_m)
     got_m = swap(send_m, 2)
     got_trace = swap(trace, 4)
-    (metric,) = whole_call(last_metric_kernel, "last_metric", (((piece, bands), bf16),))(place, keep_m, got_m)
-    ham, trace = whole_call(
-        last_ham_kernel, "last_ham", (((piece, bands), bf16), ((8, bands), f32))
-    )(place, keep_h, trace, got_trace, *got_h)
-    near = [ham] + [swap(ham, 4 * step) for step in steps]
-    pair = jnp.concatenate([metric, swap(metric, 2)])
+    both = ((2, piece, bands), bf16)
+    band, trace = whole_call(last_kernel, "last", (both, ((8, bands), f32)))(
+        place, keep_h, keep_m, got_m, trace, got_trace, *got_h
+    )
+    near = [band] + [swap(band, 4 * step) for step in steps]
+    far = [swap(part, 2) for part in near]
     bit = 8
     while bit < devices:
         trace = trace + swap(trace, bit)
         bit *= 2
-    trace = trace + swap(trace, 1)
-    far = swap(jnp.concatenate(near), 2)
-    pairs = [pair] + [swap(pair, 4 * step) for step in steps]
-
+
+    total_trace = trace + swap(trace, 1)
     factor = math.sqrt(orbitals)
+    part = ((piece, width), bf16)
+    bands_half = pltpu.VMEM((2, rows // 2, bands), bf16)
+    grads = whole_call(
+        functools.partial(chip_gradient_kernel, factor, False), "gradient_near", (part,) * lines, (bands_half,), limit=32
+    )(place, tie(prods, far[0], far[1], trace), prods_all, *near)
+    got_near = [grads[0]] + [swap(grads[step], 4 * step) for step in steps]
     *grads, matrices = whole_call(
-        functools.partial(chip_gradient_kernel, factor, lines),
-        "chip_gradient",
-        (((piece, width), bf16),) * chips + (((2, rows, bands), bf16),),
-        (pltpu.VMEM((2, bands, width), bf16), pltpu.VMEM((rows, width), bf16)),
+        functools.partial(chip_gradient_kernel, factor, True),
+        "gradient_far",
+        (part,) * lines + (((2, rows, bands), bf16),),
+        (bands_half,),
         limit=32,
-    )(place, tie(prods, trace), prods_cross, far, *near, *pairs)
-    grads = [grads[0]] + [swap(grad, 2 * step) for step, grad in enumerate(grads[1:], 1)]
+    )(place, tie(prods, total_trace, *got_near), prods_all, *far, *near)
+    got_far = [swap(grad, 4 * step + 2) for step, grad in enumerate(grads)]
+    grads = [value for pair in zip(got_near, got_far) for value in pair]
     band_hamiltonian, energy = whole_call(
         functools.partial(finish_kernel, factor, piece),
         "finish",
         (((bands, bands), f32), ((1, 1), f32)),
         (pltpu.VMEM((2, bands, bands), bf16),),
         limit=32,
-    )(place, matrices, swap(matrices, 1), trace)
+    )(place, matrices, swap(matrices, 1), total_trace)
     (gradient,) = whole_call(join_kernel, "join", (((piece, orbitals), bf16),))(
         place, tie(grads[0], energy), *grads[1:]
     )

time: 139 us -> 133 us (0.957)
  starting transfers between devices: 50.7 us -> 46 us
  waiting for transfers between devices: 51.3 us -> 48.2 us
    ppermute x39 -> x38, starting transfers between devices: 44.6 us -> 39.8 us  [swap(): return lax.ppermute(value, 'rows', [(i, i ^ bit) for i in range(count)])]
    ppermute x39 -> x38, waiting for transfers between devices: 46.5 us -> 43.4 us  [swap(): return lax.ppermute(value, 'rows', [(i, i ^ bit) for i in range(count)])]
    pallas_call x11 -> x12, Pallas kernels: 19.6 us -> 20.3 us  [call(): pl.pallas_call(kernel, out_shape=tuple((jax.ShapeDtypeStruct(shape, dtype...]
  transfers between devices with their start and end apart: 41 -> 40, of which waited for: 16 -> 16; matrix products, arithmetic and copies ran while one was open for 1% -> 1% of each run, Pallas kernels for 15% -> 16%
where the time goes in v2:
time: 133 us; the launch traced here: 132 us
  waiting for transfers between devices  48.2 us (36%)
  starting transfers between devices  46 us (35%)
  Pallas kernels  31.3 us (24%)
  local copies, waits for them, and re-layouts  4.32 us (3%)
    ppermute x38, waiting for transfers between devices, swap(): return lax.ppermute(value, 'rows', [(i, i ^ bit) for i in range(count)])  43.4 us
    ppermute x38, starting transfers between devices, swap(): return lax.ppermute(value, 'rows', [(i, i ^ bit) for i in range(count)])  39.8 us
    pallas_call x12, Pallas kernels, call(): pl.pallas_call(kernel, out_shape=tuple((jax.ShapeDtypeStruct(shape, dtype...  20.3 us
    pallas_call x2, Pallas kernels, expand_call(): pl.pallas_call(expand_own_kernel if own else expand_packed_kernel, out_sh...  11 us
    unnamed x6, local copies, waits for them, and re-layouts  4.32 us
    ppermute x1, starting transfers between devices, by_chip(): right = lax.ppermute(low, 'rows', [(i + 2, i) for i in range(devices - 2)])  4 us
    ppermute x1, waiting for transfers between devices, by_chip(): right = lax.ppermute(low, 'rows', [(i + 2, i) for i in range(devices - 2)])  3.62 us
  transfers between devices with their start and end apart: 40, of which 16 were waited for; matrix products, arithmetic and copies ran while one was open for 1% of the time, Pallas kernels for 16%

profile of v2, /device:TPU:9, one launch (start us, length us, event | category | flops | bytes accessed | tf_op | source)
XLA Modules:
  0.0 131.5 jit_solution(8335487305865291020)
XLA Ops:
  0.8 1.1 copy-done.2
  1.9 0.6 split.1
  2.5 1.3 collective-permute-start
  4.0 1.2 collective-permute-start.2
  5.2 2.3 %collective-permute-start.3 = (bf16[48,1024]{1,0:T(8,128)(2,1)S(1)}, bf16[48,1024]{1,0:T(8,128)(2,1)S(1)}, u32[]{:S(2)}, u32[]{:S(2)}) collective-permute-start(bf16[48,1024]{1,0:T(8,128)(2,1)S(1)} %get-tuple-element.66), channel_id=1, source_target_pairs={{0,8},{1,9},{2,10},{3,11},{4,12},{5,13},{6,14},{7,15},{8,0},{9,1},... | collective-permute-start | bytes 294920 | tf_op jit(solution)/shard_map/ppermute | solution.py:136
  7.5 1.0 collective-permute-start.4
  8.5 1.3 collective-permute-start.5
  10.0 0.8 fusion.cols_ref
  10.7 1.6 %copy-done = bf16[8,16,64,64]{3,2,1,0:T(8,128)(2,1)S(1)} copy-done((bf16[8,16,64,64]{3,2,1,0:T(8,128)(2,1)S(1)}, bf16[8,16,64,64]{3,2,1,0:T(8,128)(2,1)}, u32[]{:S(2)}) %copy-start) | copy-done | bytes 1048600
  12.3 1.6 %copy-done.1 = bf16[8,16,64,64]{3,2,1,0:T(8,128)(2,1)S(1)} copy-done((bf16[8,16,64,64]{3,2,1,0:T(8,128)(2,1)S(1)}, bf16[8,16,64,64]{3,2,1,0:T(8,128)(2,1)}, u32[]{:S(2)}) %copy-start.1) | copy-done | bytes 1048600
  13.9 5.7 %expand_own.1 = (bf16[2,2,512,1024]{3,2,1,0:T(8,128)(2,1)S(1)}, bf16[2,2,512,512]{3,2,1,0:T(8,128)(2,1)S(1)}, bf16[2,8,8,64,128]{4,3,2,1,0:T(8,128)(2,1)S(1)}) custom-call(s32[8,16]{1,0:T(8,128)S(1)} %fusion.cols_ref, bf16[8,16,64,64]{3,2,1,0:T(8,128)(2,1)S(1)} %copy-done, bf16[8,16,64,64]{3,2,1,0:T(8,128)(2,1)S(1)} %copy-done.1), custom_call_target="tpu_custom_call" | custom-call | bytes 1024 | tf_op jit(solution)/shard_map/expand_own/pallas_call | solution.py:194
  19.6 2.4 %collective-permute-done.5.refs_6_ = bf16[48,1024]{1,0:T(8,128)(2,1)S(1)} collective-permute-done((bf16[48,1024]{1,0:T(8,128)(2,1)S(1)}, bf16[48,1024]{1,0:T(8,128)(2,1)S(1)}, u32[]{:S(2)}, u32[]{:S(2)}) %collective-permute-start.5) | collective-permute-done | bytes 98336 | tf_op jit(solution)/shard_map/ppermute | solution.py:136
  22.0 3.7 %collective-permute-done.6.refs_7_ = bf16[48,1024]{1,0:T(8,128)(2,1)S(1)} collective-permute-done((bf16[48,1024]{1,0:T(8,128)(2,1)S(1)}, bf16[48,1024]{1,0:T(8,128)(2,1)S(1)}, u32[]{:S(2)}, u32[]{:S(2)}) %collective-permute-start.6) | collective-permute-done | bytes 98336 | tf_op jit(solution)/shard_map/ppermute | solution.py:136
  25.7 0.6 stack.21
  26.4 1.2 collective-permute-start.9
  27.7 2.2 %collective-permute-start.10 = (bf16[384,512]{1,0:T(8,128)(2,1)S(1)}, bf16[384,512]{1,0:T(8,128)(2,1)S(1)}, u32[]{:S(2)}, u32[]{:S(2)}) collective-permute-start(bf16[384,512]{1,0:T(8,128)(2,1)S(1)} %get-tuple-element.76), channel_id=1, source_target_pairs={{0,2},{1,3},{2,4},{3,5},{4,6},{5,7},{6,8},{7,9},{8,10},{9,11},{10,... | collective-permute-start | bytes 1179656 | tf_op jit(solution)/shard_map/ppermute | solution.py:434
  29.9 4.0 %collective-permute-start.11 = (bf16[384,512]{1,0:T(8,128)(2,1)S(1)}, bf16[384,512]{1,0:T(8,128)(2,1)S(1)}, u32[]{:S(2)}, u32[]{:S(2)}) collective-permute-start(bf16[384,512]{1,0:T(8,128)(2,1)S(1)} %get-tuple-element.77), channel_id=1, source_target_pairs={{2,0},{3,1},{4,2},{5,3},{6,4},{7,5},{8,6},{9,7},{10,8},{11,9},{12,... | collective-permute-start | bytes 1179656 | tf_op jit(solution)/shard_map/ppermute | solution.py:435
  33.9 1.1 collective-permute-start.8
  35.0 0.8 collective-permute-done.8.cols_ref
  35.8 5.3 %expand_packed.1 = (bf16[2,2,512,1024]{3,2,1,0:T(8,128)(2,1)S(1)}, bf16[2,2,512,512]{3,2,1,0:T(8,128)(2,1)S(1)}) custom-call(s32[8,16]{1,0:T(8,128)S(1)} %collective-permute-done.8.cols_ref, bf16[2,8,8,64,128]{4,3,2,1,0:T(8,128)(2,1)S(1)} %collective-permute-done.9.packed_ref), custom_call_target="tpu_custom_call" | custom-call | bytes 1024 | tf_op jit(solution)/shard_map/expand_packed/pallas_call | solution.py:194
  41.1 4.1 %inner.1 = (bf16[768,1024]{1,0:T(8,128)(2,1)S(1)}, f32[2,2,384,512]{3,2,1,0:T(8,128)S(1)}) custom-call(s32[4]{0:T(128)S(1)} %pad_add_fusion.place_ref, bf16[384,1024]{1,0:T(8,128)(2,1)S(1)} %get-tuple-element.70.own_ref, bf16[384,1024]{1,0:T(8,128)(2,1)S(1)} %collective-permute-done.7.cross_ref, bf16[2,2,512,1024]{3,2,1,0:T(8,128)(2,1)S(1)} %get-tuple-element.61.mine_ref, ...), custom_call_target="tpu_custom_call" | custom-call | bytes 1024 | tf_op jit(solution)/shard_map/inner/pallas_call | solution.py:230
  45.2 1.1 collective-permute-done.10.left_ref
  46.4 3.6 %collective-permute-done.11.right_ref = bf16[384,512]{1,0:T(8,128)(2,1)S(1)} collective-permute-done((bf16[384,512]{1,0:T(8,128)(2,1)S(1)}, bf16[384,512]{1,0:T(8,128)(2,1)S(1)}, u32[]{:S(2)}, u32[]{:S(2)}) %collective-permute-start.11) | collective-permute-done | bytes 393248 | tf_op jit(solution)/shard_map/ppermute | solution.py:435
  50.0 4.9 %outer.1 = (bf16[2,384,1024]{2,1,0:T(8,128)(2,1)S(1)}, f32[4,48,768]{2,1,0:T(8,128)S(1)}, bf16[4,48,768]{2,1,0:T(8,128)(2,1)S(1)}, f32[96,768]{1,0:T(8,128)S(1)}...) custom-call(s32[4]{0:T(128)S(1)} %pad_add_fusion.place_ref, ...), custom_call_target="tpu_custom_call" | custom-call | bytes 1024 | tf_op jit(solution)/shard_map/outer/pallas_call | solution.py:230
  54.9 0.5 collective-permute-start.14
  55.5 1.5 %collective-permute-start.13 = (f32[8,768]{1,0:T(8,128)S(1)}, f32[8,768]{1,0:T(8,128)S(1)}, u32[]{:S(2)}, u32[]{:S(2)}) collective-permute-start(f32[8,768]{1,0:T(8,128)S(1)} %get-tuple-element.83.trace_ref), channel_id=1, source_target_pairs={{0,2},{1,3},{2,0},{3,1},{4,6},{5,7},{6,4},{7,5},{8,10},{9,11},{10,... | collective-permute-start | bytes 73736 | tf_op jit(solution)/shard_map/ppermute | solution.py:136
  57.0 2.7 %collective-permute-start.16 = (bf16[96,768]{1,0:T(8,128)(2,1)S(1)}, bf16[96,768]{1,0:T(8,128)(2,1)S(1)}, u32[]{:S(2)}, u32[]{:S(2)}) collective-permute-start(bf16[96,768]{1,0:T(8,128)(2,1)S(1)} %get-tuple-element.88), channel_id=1, source_target_pairs={{0,8},{1,9},{2,10},{3,11},{4,12},{5,13},{6,14},{7,15},{8,0},{9,1},... | collective-permute-start | bytes 442376 | tf_op jit(solution)/shard_map/ppermute | solution.py:136
  59.6 5.0 %collective-permute-done.13.got_trace_ref = f32[8,768]{1,0:T(8,128)S(1)} collective-permute-done((f32[8,768]{1,0:T(8,128)S(1)}, f32[8,768]{1,0:T(8,128)S(1)}, u32[]{:S(2)}, u32[]{:S(2)}) %collective-permute-start.13) | collective-permute-done | bytes 24608 | tf_op jit(solution)/shard_map/ppermute | solution.py:136
  64.6 1.5 %collective-permute-start.17 = (bf16[96,768]{1,0:T(8,128)(2,1)S(1)}, bf16[96,768]{1,0:T(8,128)(2,1)S(1)}, u32[]{:S(2)}, u32[]{:S(2)}) collective-permute-start(bf16[96,768]{1,0:T(8,128)(2,1)S(1)} %get-tuple-element.89), channel_id=1, source_target_pairs={{0,12},{1,13},{2,14},{3,15},{4,8},{5,9},{6,10},{7,11},{8,4},{9,5},... | collective-permute-start | bytes 442376 | tf_op jit(solution)/shard_map/ppermute | solution.py:136
  66.1 0.6 sum_side.1
  66.7 6.8 %collective-permute-done.17.refs_2_ = bf16[96,768]{1,0:T(8,128)(2,1)S(1)} collective-permute-done((bf16[96,768]{1,0:T(8,128)(2,1)S(1)}, bf16[96,768]{1,0:T(8,128)(2,1)S(1)}, u32[]{:S(2)}, u32[]{:S(2)}) %collective-permute-start.17) | collective-permute-done | bytes 147488 | tf_op jit(solution)/shard_map/ppermute | solution.py:136
  73.5 1.5 %collective-permute-start.22 = (bf16[48,768]{1,0:T(8,128)(2,1)S(1)}, bf16[48,768]{1,0:T(8,128)(2,1)S(1)}, u32[]{:S(2)}, u32[]{:S(2)}) collective-permute-start(bf16[48,768]{1,0:T(8,128)(2,1)S(1)} %get-tuple-element.98), channel_id=1, source_target_pairs={{0,12},{1,13},{2,14},{3,15},{4,8},{5,9},{6,10},{7,11},{8,4},{9,5},... | collective-permute-start | bytes 221192 | tf_op jit(solution)/shard_map/ppermute | solution.py:136
  75.0 1.2 collective-permute-start.20
  76.2 0.8 interleave.1.all_ref
  76.9 0.6 sum_lines.1
  77.7 0.3 collective-permute-start.19
  78.0 2.8 %collective-permute-done.19.got_trace_ref = f32[8,768]{1,0:T(8,128)S(1)} collective-permute-done((f32[8,768]{1,0:T(8,128)S(1)}, f32[8,768]{1,0:T(8,128)S(1)}, u32[]{:S(2)}, u32[]{:S(2)}) %collective-permute-start.19) | collective-permute-done | bytes 24608 | tf_op jit(solution)/shard_map/ppermute | solution.py:136
  80.9 0.6 last.1
  81.5 1.0 collective-permute-start.24
  82.5 1.5 %collective-permute-start.28 = (bf16[2,48,768]{2,1,0:T(8,128)(2,1)S(1)}, bf16[2,48,768]{2,1,0:T(8,128)(2,1)S(1)}, u32[]{:S(2)}, u32[]{:S(2)}) collective-permute-start(bf16[2,48,768]{2,1,0:T(8,128)(2,1)S(1)} %get-tuple-element.99.refs_0_.refs_4_), channel_id=1, source_target_pairs={{0,12},{1,13},{2,14},{3,15},{4,8},{5,9},{6,10},{7,11},{8,4},{9,5},... | collective-permute-start | bytes 442376 | tf_op jit(solution)/shard_map/ppermute | solution.py:136
  84.0 1.1 collective-permute-start.27
  85.2 0.9 collective-permute-start.23
  86.0 0.6 collective-permute-start.25
  86.6 1.8 %collective-permute-start.26 = (f32[8,768]{1,0:T(8,128)S(1)}, f32[8,768]{1,0:T(8,128)S(1)}, u32[]{:S(2)}, u32[]{:S(2)}) collective-permute-start(f32[8,768]{1,0:T(8,128)S(1)} %get-tuple-element.100), channel_id=1, source_target_pairs={{0,8},{1,9},{2,10},{3,11},{4,12},{5,13},{6,14},{7,15},{8,0},{9,1},... | collective-permute-start | bytes 73736 | tf_op jit(solution)/shard_map/ppermute | solution.py:136
  88.4 0.8 collective-permute-start.34
  89.2 6.6 %collective-permute-done.27.refs_2_.refs_6_ = bf16[2,48,768]{2,1,0:T(8,128)(2,1)S(1)} collective-permute-done((bf16[2,48,768]{2,1,0:T(8,128)(2,1)S(1)}, bf16[2,48,768]{2,1,0:T(8,128)(2,1)S(1)}, u32[]{:S(2)}, u32[]{:S(2)}) %collective-permute-start.27) | collective-permute-done | bytes 147488 | tf_op jit(solution)/shard_map/ppermute | solution.py:136
  95.8 0.7 collective-permute-start.33
  96.6 2.9 %collective-permute-start.29 = (f32[8,768]{1,0:T(8,128)S(1)}, f32[8,768]{1,0:T(8,128)S(1)}, u32[]{:S(2)}, u32[]{:S(2)}) collective-permute-start(f32[8,768]{1,0:T(8,128)S(1)} %add.25), channel_id=1, source_target_pairs={{0,1},{1,0},{2,3},{3,2},{4,5},{5,4},{6,7},{7,6},{8,9},{9,8},{10,11... | collective-permute-start | bytes 73736 | tf_op jit(solution)/shard_map/ppermute | solution.py:136
  99.5 1.3 %gradient_near.1 = (bf16[48,1024]{1,0:T(8,128)(2,1)S(1)}, bf16[48,1024]{1,0:T(8,128)(2,1)S(1)}, bf16[48,1024]{1,0:T(8,128)(2,1)S(1)}, bf16[48,1024]{1,0:T(8,128)(2,1)S(1)}) custom-call(s32[4]{0:T(128)S(1)} %pad_add_fusion.place_ref, bf16[2,384,1024]{2,1,0:T(8,128)(2,1)S(1)} %get-tuple-element.106.mine_ref.prods_ref, ...), custom_call_target="tpu_custom_call" | custom-call | bytes 1024 | tf_op jit(solution)/shard_map/gradient_near/pallas_call | solution.py:230
  100.8 2.6 %collective-permute-start.30 = (bf16[48,1024]{1,0:T(8,128)(2,1)S(1)}, bf16[48,1024]{1,0:T(8,128)(2,1)S(1)}, u32[]{:S(2)}, u32[]{:S(2)}) collective-permute-start(bf16[48,1024]{1,0:T(8,128)(2,1)S(1)} %get-tuple-element.103), channel_id=1, source_target_pairs={{0,4},{1,5},{2,6},{3,7},{4,0},{5,1},{6,2},{7,3},{8,12},{9,13},{10,... | collective-permute-start | bytes 294920 | tf_op jit(solution)/shard_map/ppermute | solution.py:136
  103.4 0.6 collective-permute-start.31
  104.1 0.6 collective-permute-start.32
  104.7 2.2 %collective-permute-done.30.refs_2_ = bf16[48,1024]{1,0:T(8,128)(2,1)S(1)} collective-permute-done((bf16[48,1024]{1,0:T(8,128)(2,1)S(1)}, bf16[48,1024]{1,0:T(8,128)(2,1)S(1)}, u32[]{:S(2)}, u32[]{:S(2)}) %collective-permute-start.30) | collective-permute-done | bytes 98336 | tf_op jit(solution)/shard_map/ppermute | solution.py:136
  107.0 3.5 %collective-permute-done.31.refs_4_ = bf16[48,1024]{1,0:T(8,128)(2,1)S(1)} collective-permute-done((bf16[48,1024]{1,0:T(8,128)(2,1)S(1)}, bf16[48,1024]{1,0:T(8,128)(2,1)S(1)}, u32[]{:S(2)}, u32[]{:S(2)}) %collective-permute-start.31) | collective-permute-done | bytes 98336 | tf_op jit(solution)/shard_map/ppermute | solution.py:136
  110.4 3.6 %collective-permute-done.32.refs_6_ = bf16[48,1024]{1,0:T(8,128)(2,1)S(1)} collective-permute-done((bf16[48,1024]{1,0:T(8,128)(2,1)S(1)}, bf16[48,1024]{1,0:T(8,128)(2,1)S(1)}, u32[]{:S(2)}, u32[]{:S(2)}) %collective-permute-start.32) | collective-permute-done | bytes 98336 | tf_op jit(solution)/shard_map/ppermute | solution.py:136
  114.0 1.4 %gradient_far.1 = (bf16[48,1024]{1,0:T(8,128)(2,1)S(1)}, bf16[48,1024]{1,0:T(8,128)(2,1)S(1)}, bf16[48,1024]{1,0:T(8,128)(2,1)S(1)}, bf16[48,1024]{1,0:T(8,128)(2,1)S(1)}, bf16[2,384,768]{2,1,0:T(8,128)(2,1)S(1)}) custom-call(s32[4]{0:T(128)S(1)} %pad_add_fusion.place_ref, bf16[2,384,1024]{2,1,0:T(8,128)(2,1)S(1)} %get-tuple-element.106.mine_ref.prods_ref, ...), custom_call_target="tpu_custom_call" | custom-call | bytes 1024 | tf_op jit(solution)/shard_map/gradient_far/pallas_call | solution.py:230
  115.4 0.9 collective-permute-start.35
  116.6 0.4 collective-permute-start.37
  117.0 2.9 %collective-permute-start.38 = (bf16[48,1024]{1,0:T(8,128)(2,1)S(1)}, bf16[48,1024]{1,0:T(8,128)(2,1)S(1)}, u32[]{:S(2)}, u32[]{:S(2)}) collective-permute-start(bf16[48,1024]{1,0:T(8,128)(2,1)S(1)} %get-tuple-element.112), channel_id=1, source_target_pairs={{0,10},{1,11},{2,8},{3,9},{4,14},{5,15},{6,12},{7,13},{8,2},{9,3},... | collective-permute-start | bytes 294920 | tf_op jit(solution)/shard_map/ppermute | solution.py:136
  119.9 1.1 collective-permute-start.39
  121.1 3.2 %finish.1 = (f32[768,768]{1,0:T(8,128)}, f32[1,1]{1,0:T(1,128)}) custom-call(s32[4]{0:T(128)S(1)} %pad_add_fusion.place_ref, bf16[2,384,768]{2,1,0:T(8,128)(2,1)S(1)} %get-tuple-element.107.mine_ref, bf16[2,384,768]{2,1,0:T(8,128)(2,1)S(1)} %collective-permute-done.35.cross_ref, f32[8,768]{1,0:T(8,128)S(1)} %add.26.trace_ref), custom_call_target="tpu_custom_call" | custom-call | bytes 1024 | tf_op jit(solution)/shard_map/finish/pallas_call | solution.py:230
  124.3 1.7 %collective-permute-done.38.refs_5_ = bf16[48,1024]{1,0:T(8,128)(2,1)S(1)} collective-permute-done((bf16[48,1024]{1,0:T(8,128)(2,1)S(1)}, bf16[48,1024]{1,0:T(8,128)(2,1)S(1)}, u32[]{:S(2)}, u32[]{:S(2)}) %collective-permute-start.38) | collective-permute-done | bytes 98336 | tf_op jit(solution)/shard_map/ppermute | solution.py:136
  126.0 4.0 %collective-permute-done.39.refs_7_ = bf16[48,1024]{1,0:T(8,128)(2,1)S(1)} collective-permute-done((bf16[48,1024]{1,0:T(8,128)(2,1)S(1)}, bf16[48,1024]{1,0:T(8,128)(2,1)S(1)}, u32[]{:S(2)}, u32[]{:S(2)}) %collective-permute-start.39) | collective-permute-done | bytes 98336 | tf_op jit(solution)/shard_map/ppermute | solution.py:136
  130.1 1.5 %join.1 = bf16[48,8192]{1,0:T(8,128)(2,1)} custom-call(s32[4]{0:T(128)S(1)} %pad_add_fusion.place_ref, bf16[48,1024]{1,0:T(8,128)(2,1)S(1)} %get-tuple-element.109.refs_0_, bf16[48,1024]{1,0:T(8,128)(2,1)S(1)} %collective-permute-done.36.refs_1_, bf16[48,1024]{1,0:T(8,128)(2,1)S(1)} %collective-permute-done.30.refs_2_, ...), custom_call_target="tpu_custom_call" | custom-call | bytes 1024 | tf_op jit(solution)/shard_map/join/pallas_call | solution.py:230
  (40 shorter events, 1.1 us)
Async XLA Ops:
  0.8 1.1 copy-start.2
  2.5 6.0 %collective-permute-start = (bf16[48,1024]{1,0:T(8,128)(2,1)S(1)}, bf16[48,1024]{1,0:T(8,128)(2,1)S(1)}, u32[]{:S(2)}, u32[]{:S(2)}) collective-permute-start(bf16[48,1024]{1,0:T(8,128)(2,1)S(1)} %get-tuple-element.63), channel_id=1, source_target_pairs={{0,2},{1,3},{2,0},{3,1},{4,6},{5,7},{6,4},{7,5},{8,10},{9,11},{10,... | collective-permute-start | bytes 294920 | tf_op jit(solution)/shard_map/ppermute | solution.py:136
  3.8 6.0 %collective-permute-start.1 = (bf16[48,1024]{1,0:T(8,128)(2,1)S(1)}, bf16[48,1024]{1,0:T(8,128)(2,1)S(1)}, u32[]{:S(2)}, u32[]{:S(2)}) collective-permute-start(bf16[48,1024]{1,0:T(8,128)(2,1)S(1)} %get-tuple-element.64), channel_id=1, source_target_pairs={{0,4},{1,5},{2,6},{3,7},{4,0},{5,1},{6,2},{7,3},{8,12},{9,13},{10,... | collective-permute-start | bytes 294920 | tf_op jit(solution)/shard_map/ppermute | solution.py:136
  4.0 15.6 %collective-permute-start.2 = (bf16[48,1024]{1,0:T(8,128)(2,1)S(1)}, bf16[48,1024]{1,0:T(8,128)(2,1)S(1)}, u32[]{:S(2)}, u32[]{:S(2)}) collective-permute-start(bf16[48,1024]{1,0:T(8,128)(2,1)S(1)} %get-tuple-element.65), channel_id=1, source_target_pairs={{0,6},{1,7},{2,4},{3,5},{4,2},{5,3},{6,0},{7,1},{8,14},{9,15},{10,... | collective-permute-start | bytes 294920 | tf_op jit(solution)/shard_map/ppermute | solution.py:136
  5.2 14.4 %collective-permute-start.3 = (bf16[48,1024]{1,0:T(8,128)(2,1)S(1)}, bf16[48,1024]{1,0:T(8,128)(2,1)S(1)}, u32[]{:S(2)}, u32[]{:S(2)}) collective-permute-start(bf16[48,1024]{1,0:T(8,128)(2,1)S(1)} %get-tuple-element.66), channel_id=1, source_target_pairs={{0,8},{1,9},{2,10},{3,11},{4,12},{5,13},{6,14},{7,15},{8,0},{9,1},... | collective-permute-start | bytes 294920 | tf_op jit(solution)/shard_map/ppermute | solution.py:136
  7.5 12.1 %collective-permute-start.4 = (bf16[48,1024]{1,0:T(8,128)(2,1)S(1)}, bf16[48,1024]{1,0:T(8,128)(2,1)S(1)}, u32[]{:S(2)}, u32[]{:S(2)}) collective-permute-start(bf16[48,1024]{1,0:T(8,128)(2,1)S(1)} %get-tuple-element.67), channel_id=1, source_target_pairs={{0,10},{1,11},{2,8},{3,9},{4,14},{5,15},{6,12},{7,13},{8,2},{9,3},... | collective-permute-start | bytes 294920 | tf_op jit(solution)/shard_map/ppermute | solution.py:136
  8.5 13.5 %collective-permute-start.5 = (bf16[48,1024]{1,0:T(8,128)(2,1)S(1)}, bf16[48,1024]{1,0:T(8,128)(2,1)S(1)}, u32[]{:S(2)}, u32[]{:S(2)}) collective-permute-start(bf16[48,1024]{1,0:T(8,128)(2,1)S(1)} %get-tuple-element.68), channel_id=1, source_target_pairs={{0,12},{1,13},{2,14},{3,15},{4,8},{5,9},{6,10},{7,11},{8,4},{9,5},... | collective-permute-start | bytes 294920 | tf_op jit(solution)/shard_map/ppermute | solution.py:136
  9.8 15.9 %collective-permute-start.6 = (bf16[48,1024]{1,0:T(8,128)(2,1)S(1)}, bf16[48,1024]{1,0:T(8,128)(2,1)S(1)}, u32[]{:S(2)}, u32[]{:S(2)}) collective-permute-start(bf16[48,1024]{1,0:T(8,128)(2,1)S(1)} %get-tuple-element.69), channel_id=1, source_target_pairs={{0,14},{1,15},{2,12},{3,13},{4,10},{5,11},{6,8},{7,9},{8,6},{9,7},... | collective-permute-start | bytes 294920 | tf_op jit(solution)/shard_map/ppermute | solution.py:136
  10.7 1.6 %copy-start = (bf16[8,16,64,64]{3,2,1,0:T(8,128)(2,1)S(1)}, bf16[8,16,64,64]{3,2,1,0:T(8,128)(2,1)}, u32[]{:S(2)}) copy-start(bf16[8,16,64,64]{3,2,1,0:T(8,128)(2,1)} %ham_ref.1) | copy-start | bytes 3145732
  12.3 1.6 %copy-start.1 = (bf16[8,16,64,64]{3,2,1,0:T(8,128)(2,1)S(1)}, bf16[8,16,64,64]{3,2,1,0:T(8,128)(2,1)}, u32[]{:S(2)}) copy-start(bf16[8,16,64,64]{3,2,1,0:T(8,128)(2,1)} %metric_ref.1) | copy-start | bytes 3145732
  26.4 9.4 %collective-permute-start.9 = (bf16[2,8,8,64,128]{4,3,2,1,0:T(8,128)(2,1)S(1)}, bf16[2,8,8,64,128]{4,3,2,1,0:T(8,128)(2,1)S(1)}, u32[]{:S(2)}, u32[]{:S(2)}) collective-permute-start(bf16[2,8,8,64,128]{4,3,2,1,0:T(8,128)(2,1)S(1)} %get-tuple-element.72), channel_id=1, source_target_pairs={{0,1},{1,0},{2,3},{3,2},{4,5},{5,4},{6,7},{7,6},{8,9},{9,8},{10,11... | collective-permute-start | bytes 6291464 | tf_op jit(solution)/shard_map/ppermute | solution.py:136
  27.6 13.5 %collective-permute-start.7 = (bf16[384,1024]{1,0:T(8,128)(2,1)S(1)}, bf16[384,1024]{1,0:T(8,128)(2,1)S(1)}, u32[]{:S(2)}, u32[]{:S(2)}) collective-permute-start(bf16[384,1024]{1,0:T(8,128)(2,1)S(1)} %get-tuple-element.70.own_ref), channel_id=1, source_target_pairs={{0,1},{1,0},{2,3},{3,2},{4,5},{5,4},{6,7},{7,6},{8,9},{9,8},{10,11... | collective-permute-start | bytes 2359304 | tf_op jit(solution)/shard_map/ppermute | solution.py:136
  27.7 18.6 %collective-permute-start.10 = (bf16[384,512]{1,0:T(8,128)(2,1)S(1)}, bf16[384,512]{1,0:T(8,128)(2,1)S(1)}, u32[]{:S(2)}, u32[]{:S(2)}) collective-permute-start(bf16[384,512]{1,0:T(8,128)(2,1)S(1)} %get-tuple-element.76), channel_id=1, source_target_pairs={{0,2},{1,3},{2,4},{3,5},{4,6},{5,7},{6,8},{7,9},{8,10},{9,11},{10,... | collective-permute-start | bytes 1179656 | tf_op jit(solution)/shard_map/ppermute | solution.py:434
  29.9 20.1 %collective-permute-start.11 = (bf16[384,512]{1,0:T(8,128)(2,1)S(1)}, bf16[384,512]{1,0:T(8,128)(2,1)S(1)}, u32[]{:S(2)}, u32[]{:S(2)}) collective-permute-start(bf16[384,512]{1,0:T(8,128)(2,1)S(1)} %get-tuple-element.77), channel_id=1, source_target_pairs={{2,0},{3,1},{4,2},{5,3},{6,4},{7,5},{8,6},{9,7},{10,8},{11,9},{12,... | collective-permute-start | bytes 1179656 | tf_op jit(solution)/shard_map/ppermute | solution.py:435
  33.9 1.9 %collective-permute-start.8 = (s32[8,16]{1,0:T(8,128)S(1)}, s32[8,16]{1,0:T(8,128)S(1)}, u32[]{:S(2)}, u32[]{:S(2)}) collective-permute-start(s32[8,16]{1,0:T(8,128)S(1)} %fusion.cols_ref), channel_id=1, source_target_pairs={{0,1},{1,0},{2,3},{3,2},{4,5},{5,4},{6,7},{7,6},{8,9},{9,8},{10,11... | collective-permute-start | bytes 1544 | tf_op jit(solution)/shard_map/ppermute | solution.py:136
  54.9 21.2 %collective-permute-start.14 = (bf16[2,384,1024]{2,1,0:T(8,128)(2,1)S(1)}, bf16[2,384,1024]{2,1,0:T(8,128)(2,1)S(1)}, u32[]{:S(2)}, u32[]{:S(2)}) collective-permute-start(bf16[2,384,1024]{2,1,0:T(8,128)(2,1)S(1)} %get-tuple-element.106.mine_ref.prods_ref), channel_id=1, source_target_pairs={{0,1},{1,0},{2,3},{3,2},{4,5},{5,4},{6,7},{7,6},{8,9},{9,8},{10,11... | collective-permute-start | bytes 4718600 | tf_op jit(solution)/shard_map/ppermute | solution.py:136
  55.5 10.6 %collective-permute-start.12 = (bf16[4,48,768]{2,1,0:T(8,128)(2,1)S(1)}, bf16[4,48,768]{2,1,0:T(8,128)(2,1)S(1)}, u32[]{:S(2)}, u32[]{:S(2)}) collective-permute-start(bf16[4,48,768]{2,1,0:T(8,128)(2,1)S(1)} %get-tuple-element.82), channel_id=1, source_target_pairs={{0,2},{1,3},{2,0},{3,1},{4,6},{5,7},{6,4},{7,5},{8,10},{9,11},{10,... | collective-permute-start | bytes 884744 | tf_op jit(solution)/shard_map/ppermute | solution.py:136
  55.5 9.1 %collective-permute-start.13 = (f32[8,768]{1,0:T(8,128)S(1)}, f32[8,768]{1,0:T(8,128)S(1)}, u32[]{:S(2)}, u32[]{:S(2)}) collective-permute-start(f32[8,768]{1,0:T(8,128)S(1)} %get-tuple-element.83.trace_ref), channel_id=1, source_target_pairs={{0,2},{1,3},{2,0},{3,1},{4,6},{5,7},{6,4},{7,5},{8,10},{9,11},{10,... | collective-permute-start | bytes 73736 | tf_op jit(solution)/shard_map/ppermute | solution.py:136
  57.0 9.7 %collective-permute-start.15 = (bf16[96,768]{1,0:T(8,128)(2,1)S(1)}, bf16[96,768]{1,0:T(8,128)(2,1)S(1)}, u32[]{:S(2)}, u32[]{:S(2)}) collective-permute-start(bf16[96,768]{1,0:T(8,128)(2,1)S(1)} %get-tuple-element.87), channel_id=1, source_target_pairs={{0,4},{1,5},{2,6},{3,7},{4,0},{5,1},{6,2},{7,3},{8,12},{9,13},{10,... | collective-permute-start | bytes 442376 | tf_op jit(solution)/shard_map/ppermute | solution.py:136
  57.0 9.7 %collective-permute-start.16 = (bf16[96,768]{1,0:T(8,128)(2,1)S(1)}, bf16[96,768]{1,0:T(8,128)(2,1)S(1)}, u32[]{:S(2)}, u32[]{:S(2)}) collective-permute-start(bf16[96,768]{1,0:T(8,128)(2,1)S(1)} %get-tuple-element.88), channel_id=1, source_target_pairs={{0,8},{1,9},{2,10},{3,11},{4,12},{5,13},{6,14},{7,15},{8,0},{9,1},... | collective-permute-start | bytes 442376 | tf_op jit(solution)/shard_map/ppermute | solution.py:136
  64.6 8.9 %collective-permute-start.17 = (bf16[96,768]{1,0:T(8,128)(2,1)S(1)}, bf16[96,768]{1,0:T(8,128)(2,1)S(1)}, u32[]{:S(2)}, u32[]{:S(2)}) collective-permute-start(bf16[96,768]{1,0:T(8,128)(2,1)S(1)} %get-tuple-element.89), channel_id=1, source_target_pairs={{0,12},{1,13},{2,14},{3,15},{4,8},{5,9},{6,10},{7,11},{8,4},{9,5},... | collective-permute-start | bytes 442376 | tf_op jit(solution)/shard_map/ppermute | solution.py:136
  73.5 7.4 %collective-permute-start.22 = (bf16[48,768]{1,0:T(8,128)(2,1)S(1)}, bf16[48,768]{1,0:T(8,128)(2,1)S(1)}, u32[]{:S(2)}, u32[]{:S(2)}) collective-permute-start(bf16[48,768]{1,0:T(8,128)(2,1)S(1)} %get-tuple-element.98), channel_id=1, source_target_pairs={{0,12},{1,13},{2,14},{3,15},{4,8},{5,9},{6,10},{7,11},{8,4},{9,5},... | collective-permute-start | bytes 221192 | tf_op jit(solution)/shard_map/ppermute | solution.py:136
  75.0 5.9 %collective-permute-start.21 = (bf16[48,768]{1,0:T(8,128)(2,1)S(1)}, bf16[48,768]{1,0:T(8,128)(2,1)S(1)}, u32[]{:S(2)}, u32[]{:S(2)}) collective-permute-start(bf16[48,768]{1,0:T(8,128)(2,1)S(1)} %get-tuple-element.96), channel_id=1, source_target_pairs={{0,8},{1,9},{2,10},{3,11},{4,12},{5,13},{6,14},{7,15},{8,0},{9,1},... | collective-permute-start | bytes 221192 | tf_op jit(solution)/shard_map/ppermute | solution.py:136
  75.0 5.9 %collective-permute-start.20 = (bf16[48,768]{1,0:T(8,128)(2,1)S(1)}, bf16[48,768]{1,0:T(8,128)(2,1)S(1)}, u32[]{:S(2)}, u32[]{:S(2)}) collective-permute-start(bf16[48,768]{1,0:T(8,128)(2,1)S(1)} %get-tuple-element.94), channel_id=1, source_target_pairs={{0,4},{1,5},{2,6},{3,7},{4,0},{5,1},{6,2},{7,3},{8,12},{9,13},{10,... | collective-permute-start | bytes 221192 | tf_op jit(solution)/shard_map/ppermute | solution.py:136
  77.6 3.4 %collective-permute-start.18 = (bf16[48,768]{1,0:T(8,128)(2,1)S(1)}, bf16[48,768]{1,0:T(8,128)(2,1)S(1)}, u32[]{:S(2)}, u32[]{:S(2)}) collective-permute-start(bf16[48,768]{1,0:T(8,128)(2,1)S(1)} %get-tuple-element.91), channel_id=1, source_target_pairs={{0,2},{1,3},{2,0},{3,1},{4,6},{5,7},{6,4},{7,5},{8,10},{9,11},{10,... | collective-permute-start | bytes 221192 | tf_op jit(solution)/shard_map/ppermute | solution.py:136
  77.7 3.2 %collective-permute-start.19 = (f32[8,768]{1,0:T(8,128)S(1)}, f32[8,768]{1,0:T(8,128)S(1)}, u32[]{:S(2)}, u32[]{:S(2)}) collective-permute-start(f32[8,768]{1,0:T(8,128)S(1)} %get-tuple-element.92.trace_ref), channel_id=1, source_target_pairs={{0,4},{1,5},{2,6},{3,7},{4,0},{5,1},{6,2},{7,3},{8,12},{9,13},{10,... | collective-permute-start | bytes 73736 | tf_op jit(solution)/shard_map/ppermute | solution.py:136
  81.5 4.5 %collective-permute-start.24 = (bf16[2,48,768]{2,1,0:T(8,128)(2,1)S(1)}, bf16[2,48,768]{2,1,0:T(8,128)(2,1)S(1)}, u32[]{:S(2)}, u32[]{:S(2)}) collective-permute-start(bf16[2,48,768]{2,1,0:T(8,128)(2,1)S(1)} %get-tuple-element.99.refs_0_.refs_4_), channel_id=1, source_target_pairs={{0,4},{1,5},{2,6},{3,7},{4,0},{5,1},{6,2},{7,3},{8,12},{9,13},{10,... | collective-permute-start | bytes 442376 | tf_op jit(solution)/shard_map/ppermute | solution.py:136
  82.5 5.9 %collective-permute-start.28 = (bf16[2,48,768]{2,1,0:T(8,128)(2,1)S(1)}, bf16[2,48,768]{2,1,0:T(8,128)(2,1)S(1)}, u32[]{:S(2)}, u32[]{:S(2)}) collective-permute-start(bf16[2,48,768]{2,1,0:T(8,128)(2,1)S(1)} %get-tuple-element.99.refs_0_.refs_4_), channel_id=1, source_target_pairs={{0,12},{1,13},{2,14},{3,15},{4,8},{5,9},{6,10},{7,11},{8,4},{9,5},... | collective-permute-start | bytes 442376 | tf_op jit(solution)/shard_map/ppermute | solution.py:136
  84.0 11.8 %collective-permute-start.27 = (bf16[2,48,768]{2,1,0:T(8,128)(2,1)S(1)}, bf16[2,48,768]{2,1,0:T(8,128)(2,1)S(1)}, u32[]{:S(2)}, u32[]{:S(2)}) collective-permute-start(bf16[2,48,768]{2,1,0:T(8,128)(2,1)S(1)} %get-tuple-element.99.refs_0_.refs_4_), channel_id=1, source_target_pairs={{0,8},{1,9},{2,10},{3,11},{4,12},{5,13},{6,14},{7,15},{8,0},{9,1},... | collective-permute-start | bytes 442376 | tf_op jit(solution)/shard_map/ppermute | solution.py:136
  85.2 14.3 %collective-permute-start.23 = (bf16[2,48,768]{2,1,0:T(8,128)(2,1)S(1)}, bf16[2,48,768]{2,1,0:T(8,128)(2,1)S(1)}, u32[]{:S(2)}, u32[]{:S(2)}) collective-permute-start(bf16[2,48,768]{2,1,0:T(8,128)(2,1)S(1)} %get-tuple-element.99.refs_0_.refs_4_), channel_id=1, source_target_pairs={{0,2},{1,3},{2,0},{3,1},{4,6},{5,7},{6,4},{7,5},{8,10},{9,11},{10,... | collective-permute-start | bytes 442376 | tf_op jit(solution)/shard_map/ppermute | solution.py:136
  86.0 13.4 %collective-permute-start.25 = (bf16[2,48,768]{2,1,0:T(8,128)(2,1)S(1)}, bf16[2,48,768]{2,1,0:T(8,128)(2,1)S(1)}, u32[]{:S(2)}, u32[]{:S(2)}) collective-permute-start(bf16[2,48,768]{2,1,0:T(8,128)(2,1)S(1)} %collective-permute-done.24.refs_1_.refs_5_), channel_id=1, source_target_pairs={{0,2},{1,3},{2,0},{3,1},{4,6},{5,7},{6,4},{7,5},{8,10},{9,11},{10,... | collective-permute-start | bytes 442376 | tf_op jit(solution)/shard_map/ppermute | solution.py:136
  86.6 9.9 %collective-permute-start.26 = (f32[8,768]{1,0:T(8,128)S(1)}, f32[8,768]{1,0:T(8,128)S(1)}, u32[]{:S(2)}, u32[]{:S(2)}) collective-permute-start(f32[8,768]{1,0:T(8,128)S(1)} %get-tuple-element.100), channel_id=1, source_target_pairs={{0,8},{1,9},{2,10},{3,11},{4,12},{5,13},{6,14},{7,15},{8,0},{9,1},... | collective-permute-start | bytes 73736 | tf_op jit(solution)/shard_map/ppermute | solution.py:136
  88.4 25.6 %collective-permute-start.34 = (bf16[2,48,768]{2,1,0:T(8,128)(2,1)S(1)}, bf16[2,48,768]{2,1,0:T(8,128)(2,1)S(1)}, u32[]{:S(2)}, u32[]{:S(2)}) collective-permute-start(bf16[2,48,768]{2,1,0:T(8,128)(2,1)S(1)} %collective-permute-done.28.refs_3_.refs_7_), channel_id=1, source_target_pairs={{0,2},{1,3},{2,0},{3,1},{4,6},{5,7},{6,4},{7,5},{8,10},{9,11},{10,... | collective-permute-start | bytes 442376 | tf_op jit(solution)/shard_map/ppermute | solution.py:136
  95.8 18.2 %collective-permute-start.33 = (bf16[2,48,768]{2,1,0:T(8,128)(2,1)S(1)}, bf16[2,48,768]{2,1,0:T(8,128)(2,1)S(1)}, u32[]{:S(2)}, u32[]{:S(2)}) collective-permute-start(bf16[2,48,768]{2,1,0:T(8,128)(2,1)S(1)} %collective-permute-done.27.refs_2_.refs_6_), channel_id=1, source_target_pairs={{0,2},{1,3},{2,0},{3,1},{4,6},{5,7},{6,4},{7,5},{8,10},{9,11},{10,... | collective-permute-start | bytes 442376 | tf_op jit(solution)/shard_map/ppermute | solution.py:136
  96.6 7.5 %collective-permute-start.29 = (f32[8,768]{1,0:T(8,128)S(1)}, f32[8,768]{1,0:T(8,128)S(1)}, u32[]{:S(2)}, u32[]{:S(2)}) collective-permute-start(f32[8,768]{1,0:T(8,128)S(1)} %add.25), channel_id=1, source_target_pairs={{0,1},{1,0},{2,3},{3,2},{4,5},{5,4},{6,7},{7,6},{8,9},{9,8},{10,11... | collective-permute-start | bytes 73736 | tf_op jit(solution)/shard_map/ppermute | solution.py:136
  100.8 6.1 %collective-permute-start.30 = (bf16[48,1024]{1,0:T(8,128)(2,1)S(1)}, bf16[48,1024]{1,0:T(8,128)(2,1)S(1)}, u32[]{:S(2)}, u32[]{:S(2)}) collective-permute-start(bf16[48,1024]{1,0:T(8,128)(2,1)S(1)} %get-tuple-element.103), channel_id=1, source_target_pairs={{0,4},{1,5},{2,6},{3,7},{4,0},{5,1},{6,2},{7,3},{8,12},{9,13},{10,... | collective-permute-start | bytes 294920 | tf_op jit(solution)/shard_map/ppermute | solution.py:136
  103.4 7.0 %collective-permute-start.31 = (bf16[48,1024]{1,0:T(8,128)(2,1)S(1)}, bf16[48,1024]{1,0:T(8,128)(2,1)S(1)}, u32[]{:S(2)}, u32[]{:S(2)}) collective-permute-start(bf16[48,1024]{1,0:T(8,128)(2,1)S(1)} %get-tuple-element.104), channel_id=1, source_target_pairs={{0,8},{1,9},{2,10},{3,11},{4,12},{5,13},{6,14},{7,15},{8,0},{9,1},... | collective-permute-start | bytes 294920 | tf_op jit(solution)/shard_map/ppermute | solution.py:136
  104.1 9.9 %collective-permute-start.32 = (bf16[48,1024]{1,0:T(8,128)(2,1)S(1)}, bf16[48,1024]{1,0:T(8,128)(2,1)S(1)}, u32[]{:S(2)}, u32[]{:S(2)}) collective-permute-start(bf16[48,1024]{1,0:T(8,128)(2,1)S(1)} %get-tuple-element.105), channel_id=1, source_target_pairs={{0,12},{1,13},{2,14},{3,15},{4,8},{5,9},{6,10},{7,11},{8,4},{9,5},... | collective-permute-start | bytes 294920 | tf_op jit(solution)/shard_map/ppermute | solution.py:136
  115.4 5.6 %collective-permute-start.35 = (bf16[2,384,768]{2,1,0:T(8,128)(2,1)S(1)}, bf16[2,384,768]{2,1,0:T(8,128)(2,1)S(1)}, u32[]{:S(2)}, u32[]{:S(2)}) collective-permute-start(bf16[2,384,768]{2,1,0:T(8,128)(2,1)S(1)} %get-tuple-element.107.mine_ref), channel_id=1, source_target_pairs={{0,1},{1,0},{2,3},{3,2},{4,5},{5,4},{6,7},{7,6},{8,9},{9,8},{10,11... | collective-permute-start | bytes 3538952 | tf_op jit(solution)/shard_map/ppermute | solution.py:136
  116.3 7.9 %collective-permute-start.36 = (bf16[48,1024]{1,0:T(8,128)(2,1)S(1)}, bf16[48,1024]{1,0:T(8,128)(2,1)S(1)}, u32[]{:S(2)}, u32[]{:S(2)}) collective-permute-start(bf16[48,1024]{1,0:T(8,128)(2,1)S(1)} %get-tuple-element.110), channel_id=1, source_target_pairs={{0,2},{1,3},{2,0},{3,1},{4,6},{5,7},{6,4},{7,5},{8,10},{9,11},{10,... | collective-permute-start | bytes 294920 | tf_op jit(solution)/shard_map/ppermute | solution.py:136
  116.6 7.7 %collective-permute-start.37 = (bf16[48,1024]{1,0:T(8,128)(2,1)S(1)}, bf16[48,1024]{1,0:T(8,128)(2,1)S(1)}, u32[]{:S(2)}, u32[]{:S(2)}) collective-permute-start(bf16[48,1024]{1,0:T(8,128)(2,1)S(1)} %get-tuple-element.111), channel_id=1, source_target_pairs={{0,6},{1,7},{2,4},{3,5},{4,2},{5,3},{6,0},{7,1},{8,14},{9,15},{10,... | collective-permute-start | bytes 294920 | tf_op jit(solution)/shard_map/ppermute | solution.py:136
  117.0 9.0 %collective-permute-start.38 = (bf16[48,1024]{1,0:T(8,128)(2,1)S(1)}, bf16[48,1024]{1,0:T(8,128)(2,1)S(1)}, u32[]{:S(2)}, u32[]{:S(2)}) collective-permute-start(bf16[48,1024]{1,0:T(8,128)(2,1)S(1)} %get-tuple-element.112), channel_id=1, source_target_pairs={{0,10},{1,11},{2,8},{3,9},{4,14},{5,15},{6,12},{7,13},{8,2},{9,3},... | collective-permute-start | bytes 294920 | tf_op jit(solution)/shard_map/ppermute | solution.py:136
  119.9 10.1 %collective-permute-start.39 = (bf16[48,1024]{1,0:T(8,128)(2,1)S(1)}, bf16[48,1024]{1,0:T(8,128)(2,1)S(1)}, u32[]{:S(2)}, u32[]{:S(2)}) collective-permute-start(bf16[48,1024]{1,0:T(8,128)(2,1)S(1)} %get-tuple-element.113), channel_id=1, source_target_pairs={{0,14},{1,15},{2,12},{3,13},{4,10},{5,11},{6,8},{7,9},{8,6},{9,7},... | collective-permute-start | bytes 294920 | tf_op jit(solution)/shard_map/ppermute | solution.py:136
